TPU v7x, 128 devices: a whole 4x4x4 slice. The times are simulated.
128 devices in a mesh: rt: 8 (over x, core), ct: 16 (over z, y).
Axes of the slice: x: 4, y: 4, z: 4, core: 2. Of those that a mesh axis runs over, the one named last changes fastest.
Arguments:
- children: float32 [4096, 12288], P(('rt', 'ct')), may hold values from -6 to 6
- row_map: int32 [4096], replicated, may hold values from 0 to 4095, as said below
- column_map: int32 [2, 12288], replicated, may hold values from 0 to 16383, as said below
- staircase: int32 [2, 48], replicated, may hold values from 640 to 2048, as said below
Outputs:
- factor_rows: float32 [512, 16384], P(None, 'ct')
- basis: float32 [512, 4096], P(None, 'rt')
- remainder: float32 [4096, 16384], P('rt', 'ct')
Inputs may be any that keep to these rules, and one draw needn't show every extreme that they name: `row_map`: A permutation of the front rows. Of the 32 stacked child rows in each aligned block of 32 (the rows of one device), at most 8 have front rows in any one aligned block of 512 front rows, and every such block of child rows reaches 8 for some block of front rows. `column_map`: each row is strictly increasing, begins with 0, 1, ..., 511 and ends with 16383. `staircase`: each row is nondecreasing and ends with 2048.
All inputs are finite; a program needn't handle non-finite values.
Results may differ from a plain program's by a relative error of at most 0.0003.
Values sent between devices are 32-bit elements; how exact they have to be, the bound alone decides.
A program may use at most 128 MiB of HBM per device.

v0:
```python
import jax
import jax.numpy as jnp
from jax import lax
from jax.sharding import PartitionSpec as P

FRONT_COLS = 16384
TILE = 256
ROWS_DEV = 512
PANEL = 512


highest = lax.Precision.HIGHEST


def from_root(value, axis, source):
    kept = jnp.where(lax.axis_index(axis) == source, value, 0).astype(value.dtype)
    return lax.psum(kept, axis)


def factor_panel(front_block, first_col, panel_width):
    panel_cols = lax.slice_in_dim(front_block, first_col, first_col + panel_width, axis=1)
    gram_matrix = lax.dot_general(
        panel_cols,
        panel_cols,
        (((0,), (0,)), ((), ())),
        precision=highest,
        preferred_element_type=jnp.float32,
    )
    gram_matrix = lax.psum(gram_matrix, "rt")
    lower_factor = jnp.linalg.cholesky(gram_matrix)
    basis_rows = jax.scipy.linalg.solve_triangular(lower_factor, panel_cols.T, lower=True)
    basis_rows = from_root(basis_rows, "ct", 0)
    partial_rows = jnp.dot(
        basis_rows, front_block, precision=highest, preferred_element_type=jnp.float32
    )
    factor = lax.psum(partial_rows, "rt")
    update = lax.dot_general(
        basis_rows,
        factor,
        (((0,), (0,)), ((), ())),
        precision=highest,
        preferred_element_type=jnp.float32,
    )
    return (front_block - update, basis_rows, factor)


def shards(children, row_map, column_map, staircase):
    tiles_down = lax.axis_size("rt")
    tiles_across = lax.axis_size("ct")
    source_rows = children.shape[0]
    child_cols = children.shape[1]
    total_rows = row_map.shape[0]
    child_rows = total_rows // 2
    sources = tiles_down * tiles_across
    capacity = 2 * source_rows // tiles_down
    block_cols = FRONT_COLS // tiles_across
    device_id = lax.axis_index("rt") * tiles_across + lax.axis_index("ct")
    first_row = device_id * source_rows
    which_child = first_row // child_rows
    within_child = first_row - which_child * child_rows + jnp.arange(source_rows, dtype=jnp.int32)
    target_tile = row_map // ROWS_DEV
    tile_ids = jnp.arange(tiles_down, dtype=jnp.int32)
    tile_hits = (
        target_tile.reshape(sources, source_rows)[:, :, None] == tile_ids[None, None, :]
    ).astype(jnp.int32)
    earlier = jnp.cumsum(tile_hits, axis=1) - tile_hits
    slot_of_row = jnp.sum(earlier * tile_hits, axis=2).reshape(-1)
    my_tiles = lax.dynamic_slice_in_dim(target_tile, first_row, source_rows)
    my_slots = lax.dynamic_slice_in_dim(slot_of_row, first_row, source_rows)
    slot_ids_all = jnp.arange(capacity, dtype=jnp.int32)
    matches = (my_tiles[None, None, :] == tile_ids[:, None, None]) & (
        my_slots[None, None, :] == slot_ids_all[None, :, None]
    )
    selection = matches.astype(jnp.float32)
    child_map = lax.dynamic_index_in_dim(column_map, which_child, 0, keepdims=False)
    child_stair = lax.dynamic_index_in_dim(staircase, which_child, 0, keepdims=False)
    limits = jnp.repeat(child_stair, TILE, total_repeat_length=child_cols)
    masked_rows = jnp.where(within_child[:, None] < limits[None, :], children, 0.0)
    column_slot = (
        jnp.zeros((FRONT_COLS,), jnp.int32)
        .at[child_map]
        .set(jnp.arange(child_cols, dtype=jnp.int32))
    )
    present = jnp.zeros((FRONT_COLS,), jnp.bool_).at[child_map].set(True)
    placed_cols = jnp.where(present[:, None], masked_rows.T[column_slot], 0.0)
    outgoing = lax.dot_general(
        selection,
        placed_cols,
        (((2,), (1,)), ((), ())),
        precision=highest,
        preferred_element_type=jnp.float32,
    )
    outgoing = outgoing.reshape(tiles_down, capacity, tiles_across, block_cols).transpose(
        0, 2, 1, 3
    )
    arrived = lax.all_to_all(
        outgoing.reshape(sources, capacity, block_cols),
        ("rt", "ct"),
        split_axis=0,
        concat_axis=0,
        tiled=True,
    )
    arrived = arrived.reshape(sources * capacity, block_cols)
    inverse = (
        jnp.zeros((total_rows,), jnp.int32).at[row_map].set(jnp.arange(total_rows, dtype=jnp.int32))
    )
    my_sources = lax.dynamic_slice_in_dim(inverse, lax.axis_index("rt") * ROWS_DEV, ROWS_DEV)
    slot_index = my_sources // source_rows * capacity + slot_of_row[my_sources]
    front_block = arrived[slot_index]
    basis_list = []
    rows_list = []
    for panel_index in range(PANEL // TILE):
        front_block, panel_basis, panel_rows = factor_panel(front_block, panel_index * TILE, TILE)
        basis_list.append(panel_basis)
        rows_list.append(panel_rows)
    basis_rows = jnp.concatenate(basis_list, axis=0)
    factor_rows = jnp.concatenate(rows_list, axis=0)
    return (factor_rows, basis_rows, front_block)


def solution(mesh):
    placed = (P(("rt", "ct"), None), P(), P(), P())
    return jax.shard_map(
        shards,
        mesh=mesh,
        in_specs=placed,
        out_specs=(P(None, "ct"), P(None, "rt"), P("rt", "ct")),
        check_vma=False,
    )
```

profile of v0, /device:TPU:0, one launch (start us, length us, event | category | flops | bytes accessed | tf_op | source)
XLA Modules:
  0.0 859.7 jit_solution(4052479294462246313)
XLA Ops:
  10.5 5.0 copy.22
  15.6 45.4 %scatter_custom_fusion.1 = s32[16384]{0:T(1024)S(1)} fusion(s32[12288]{0:T(1024)S(1)} %bitcast.138, s32[12288]{0:T(1024)S(1)} %iota.69, s32[]{:T(128)} %copy.63), kind=kCustom, calls=%fused_computation.71 | custom fusion | bytes 65540 | tf_op jit(solution)/shard_map/scatter | solution.py:82
  62.0 31.1 %select_select_fusion.2 = s32[12288]{0:T(1024)S(1)} fusion(pred[12288]{0:T(1024)(128)(4,1)S(1)} %copy-done.10, pred[12288]{0:T(1024)(128)(4,1)S(1)} %copy-done.11, pred[12288]{0:T(1024)(128)(4,1)S(1)} %copy-done.12, pred[12288]{0:T(1024)(128)(4,1)S(1)} %copy-done.13, pred[12288]{0:T(1024)(128)(4,1)S(1)} %copy-done.14, pred[12288]{0:T(1024)(128)(4,1)S(1)} %copy-done.15, ...), kind=kLoop, calls=%fused_computation.70 | loop fusion | flops 577536 | bytes 626880 | tf_op jit(solution)/shard_map/jit(_take)/gather | solution.py:77
  93.0 9.8 %select_bitcast_fusion = f32[12288,32]{1,0:T(8,128)} fusion(f32[32,12288]{0,1:T(8,128)} %copy.22, s32[32]{0:T(128)S(1)} %iota_add_fusion, s32[12288]{0:T(1024)S(1)} %select_select_fusion.2), kind=kLoop, calls=%fused_computation.13 | loop fusion | flops 786432 | bytes 3195008 | tf_op jit(solution)/shard_map/transpose | solution.py:85
  102.9 57.3 %gather_fusion = f32[16384,32]{1,0:T(8,128)} fusion(f32[12288,32]{1,0:T(8,128)} %select_bitcast_fusion, s32[16384]{0:T(1024)S(1)} %fusion.15), kind=kCustom, calls=%fused_computation | custom fusion | bytes 4259840 | tf_op jit(solution)/shard_map/gather | solution.py:85
  160.1 51.6 %scatter_custom_fusion = pred[16384]{0:T(1024)(128)(4,1)S(1)} fusion(s32[12288]{0:T(1024)S(1)} %bitcast.139, pred[12288]{0:T(1024)(128)(4,1)S(1)} %broadcast.353, pred[]{:T(512)} %constant.234.clone.1), kind=kCustom, calls=%fused_computation.73 | custom fusion | bytes 16385 | tf_op jit(solution)/shard_map/scatter | solution.py:84
  211.8 9.6 %fusion = f32[8,8,16384]{2,1,0:T(8,128)} fusion(f32[16384,32]{1,0:T(8,128)} %gather_fusion, pred[16384]{0:T(1024)(128)(4,1)S(1)} %scatter_custom_fusion, pred[8,32]{1,0:T(8,128)(4,1)S(1)} %get-tuple-element.115, pred[8,32]{1,0:T(8,128)(4,1)S(1)} %get-tuple-element.116), kind=kOutput, calls=%fused_computation.10 | convolution fusion | flops 403179520 | bytes 6308352 | tf_op jit(solution)/shard_map/dot_general | solution.py:86
  221.4 11.7 %all-to-all-start = ((f32[128,8,1024]{2,1,0:T(8,128)}), f32[128,8,1024]{2,1,0:T(8,128)}, u32[]{:S(2)}, u32[]{:S(2)}) async-start(f32[128,8,1024]{2,1,0:T(8,128)} %bitcast.135), calls=%async_computation | async-start | bytes 8388608 | tf_op jit(solution)/shard_map/all_to_all | solution.py:96
  233.1 15.7 %scatter_custom_fusion.2 = s32[4096]{0:T(1024)S(1)} fusion(s32[4096]{0:T(1024)S(1)} %get-tuple-element.61, s32[4096]{0:T(1024)S(1)} %iota.70, s32[]{:T(128)} %copy.63), kind=kCustom, calls=%fused_computation.86 | custom fusion | bytes 16388 | tf_op jit(solution)/shard_map/scatter | solution.py:105
  248.9 3.1 gather_fusion.1
  252.2 32.3 %all-to-all-done = f32[128,8,1024]{2,1,0:T(8,128)} async-done(((f32[128,8,1024]{2,1,0:T(8,128)}), f32[128,8,1024]{2,1,0:T(8,128)}, u32[]{:S(2)}, u32[]{:S(2)}) %all-to-all-start) | async-done | bytes 4194336 | tf_op jit(solution)/shard_map/all_to_all | solution.py:96
  284.5 5.0 gather_fusion.2
  291.6 56.4 %all-reduce.8.cloned.1.call-done = f32[256,256]{0,1:T(8,128)} async-done(((f32[256,256]{0,1:T(8,128)}), f32[256,256]{0,1:T(8,128)}) %all-reduce.8.cloned.1.call-update) | async-done | bytes 262160 | tf_op jit(solution)/shard_map/psum | solution.py:29
  350.1 11.7 %cholesky.130 = f32[128,128]{1,0:T(8,128)S(1)} custom-call(f32[128,128]{1,0:T(8,128)S(1)} %cholesky.194), custom_call_target="Cholesky" | custom-call | tf_op jit(solution)/shard_map/jit(cholesky)/cholesky | solution.py:30
  361.8 9.8 %custom-call.13 = f32[1,128,128]{1,2,0:T(8,128)S(1)} custom-call(f32[1,128,128]{2,1,0:T(8,128)S(1)} %get-tuple-element.60), custom_call_target="InvertDiagBlocksLowerTriangular" | custom-call | tf_op jit(solution)/shard_map/jit(cholesky)/cholesky | solution.py:30
  372.1 11.7 %cholesky.147 = f32[128,128]{1,0:T(8,128)S(1)} custom-call(f32[128,128]{1,0:T(8,128)S(1)} %convolution_subtract_fusion.5), custom_call_target="Cholesky" | custom-call | tf_op jit(solution)/shard_map/jit(cholesky)/cholesky | solution.py:30
  386.6 4.2 while.5
  390.8 19.7 %custom-call.14 = f32[2,128,128]{1,2,0:T(8,128)S(1)} custom-call(f32[2,128,128]{2,1,0:T(8,128)S(1)} %get-tuple-element.31), custom_call_target="InvertDiagBlocksLowerTriangular" | custom-call | tf_op jit(solution)/shard_map/jit(_solve_triangular)/triangular_solve | solution.py:31
  412.6 84.9 %all-reduce.10.cloned.1.call-done = f32[256,512]{1,0:T(8,128)} async-done(((f32[256,512]{1,0:T(8,128)}), f32[256,512]{1,0:T(8,128)}) %all-reduce.10.cloned.1.call-update) | async-done | bytes 524304 | tf_op jit(solution)/shard_map/psum | solution.py:17
  497.5 4.0 fusion.51
  501.6 61.9 %all-reduce.12.cloned.1.call-done = f32[256,1024]{1,0:T(8,128)} async-done(((f32[256,1024]{1,0:T(8,128)}), f32[256,1024]{1,0:T(8,128)}) %all-reduce.12.cloned.1.call-update) | async-done | bytes 1048592 | tf_op jit(solution)/shard_map/psum | solution.py:36
  563.5 3.2 convolution_subtract_fusion.1
  571.3 58.2 %all-reduce.14.cloned.1.call-done = f32[256,256]{0,1:T(8,128)} async-done(((f32[256,256]{0,1:T(8,128)}), f32[256,256]{0,1:T(8,128)}) %all-reduce.14.cloned.1.call-update) | async-done | bytes 262160 | tf_op jit(solution)/shard_map/psum | solution.py:29
  631.6 11.7 %cholesky.164 = f32[128,128]{1,0:T(8,128)S(1)} custom-call(f32[128,128]{1,0:T(8,128)S(1)} %cholesky.197), custom_call_target="Cholesky" | custom-call | tf_op jit(solution)/shard_map/jit(cholesky)/cholesky | solution.py:30
  643.4 9.8 %custom-call.15 = f32[1,128,128]{1,2,0:T(8,128)S(1)} custom-call(f32[1,128,128]{2,1,0:T(8,128)S(1)} %get-tuple-element.56), custom_call_target="InvertDiagBlocksLowerTriangular" | custom-call | tf_op jit(solution)/shard_map/jit(cholesky)/cholesky | solution.py:30
  653.7 11.7 %cholesky.181 = f32[128,128]{1,0:T(8,128)S(1)} custom-call(f32[128,128]{1,0:T(8,128)S(1)} %convolution_subtract_fusion.4), custom_call_target="Cholesky" | custom-call | tf_op jit(solution)/shard_map/jit(cholesky)/cholesky | solution.py:30
  668.0 4.0 while.6
  672.7 20.5 %custom-call.16 = f32[2,128,128]{1,2,0:T(8,128)S(1)} custom-call(f32[2,128,128]{2,1,0:T(8,128)} %copy-done.7), custom_call_target="InvertDiagBlocksLowerTriangular" | custom-call | tf_op jit(solution)/shard_map/jit(_solve_triangular)/triangular_solve | solution.py:31
  695.5 85.1 %all-reduce.16.cloned.1.call-done = f32[256,512]{1,0:T(8,128)} async-done(((f32[256,512]{1,0:T(8,128)}), f32[256,512]{1,0:T(8,128)}) %all-reduce.16.cloned.1.call-update) | async-done | bytes 524304 | tf_op jit(solution)/shard_map/psum | solution.py:17
  780.6 4.0 fusion.52
  785.7 60.9 %all-reduce.18.cloned.1.call-done = f32[256,1024]{1,0:T(8,128)} async-done(((f32[256,1024]{1,0:T(8,128)}), f32[256,1024]{1,0:T(8,128)}) %all-reduce.18.cloned.1.call-update) | async-done | bytes 1048592 | tf_op jit(solution)/shard_map/psum | solution.py:36
  846.6 4.7 convolution_subtract_fusion
  (184 shorter events, 33.9 us)
Async XLA Ops:
  10.0 51.6 %copy-start.10 = (pred[12288]{0:T(1024)(128)(4,1)S(1)}, pred[12288]{0:T(1024)(128)(4,1)}, u32[]{:S(2)}) copy-start(pred[12288]{0:T(1024)(128)(4,1)} %constant.319) | copy-start | bytes 36868
  10.0 51.6 %copy-start.11 = (pred[12288]{0:T(1024)(128)(4,1)S(1)}, pred[12288]{0:T(1024)(128)(4,1)}, u32[]{:S(2)}) copy-start(pred[12288]{0:T(1024)(128)(4,1)} %constant.320) | copy-start | bytes 36868
  10.0 51.6 %copy-start.12 = (pred[12288]{0:T(1024)(128)(4,1)S(1)}, pred[12288]{0:T(1024)(128)(4,1)}, u32[]{:S(2)}) copy-start(pred[12288]{0:T(1024)(128)(4,1)} %constant.321) | copy-start | bytes 36868
  10.1 51.6 %copy-start.13 = (pred[12288]{0:T(1024)(128)(4,1)S(1)}, pred[12288]{0:T(1024)(128)(4,1)}, u32[]{:S(2)}) copy-start(pred[12288]{0:T(1024)(128)(4,1)} %constant.322) | copy-start | bytes 36868
  10.1 51.6 %copy-start.14 = (pred[12288]{0:T(1024)(128)(4,1)S(1)}, pred[12288]{0:T(1024)(128)(4,1)}, u32[]{:S(2)}) copy-start(pred[12288]{0:T(1024)(128)(4,1)} %constant.323) | copy-start | bytes 36868
  10.1 51.6 %copy-start.15 = (pred[12288]{0:T(1024)(128)(4,1)S(1)}, pred[12288]{0:T(1024)(128)(4,1)}, u32[]{:S(2)}) copy-start(pred[12288]{0:T(1024)(128)(4,1)} %constant.324) | copy-start | bytes 36868
  10.1 51.6 %copy-start.16 = (pred[12288]{0:T(1024)(128)(4,1)S(1)}, pred[12288]{0:T(1024)(128)(4,1)}, u32[]{:S(2)}) copy-start(pred[12288]{0:T(1024)(128)(4,1)} %constant.325) | copy-start | bytes 36868
  10.1 51.6 %copy-start.17 = (pred[12288]{0:T(1024)(128)(4,1)S(1)}, pred[12288]{0:T(1024)(128)(4,1)}, u32[]{:S(2)}) copy-start(pred[12288]{0:T(1024)(128)(4,1)} %constant.326) | copy-start | bytes 36868
  10.1 51.6 %copy-start.18 = (pred[12288]{0:T(1024)(128)(4,1)S(1)}, pred[12288]{0:T(1024)(128)(4,1)}, u32[]{:S(2)}) copy-start(pred[12288]{0:T(1024)(128)(4,1)} %constant.327) | copy-start | bytes 36868
  10.1 51.6 %copy-start.19 = (pred[12288]{0:T(1024)(128)(4,1)S(1)}, pred[12288]{0:T(1024)(128)(4,1)}, u32[]{:S(2)}) copy-start(pred[12288]{0:T(1024)(128)(4,1)} %constant.328) | copy-start | bytes 36868
  10.1 51.5 %copy-start.20 = (pred[12288]{0:T(1024)(128)(4,1)S(1)}, pred[12288]{0:T(1024)(128)(4,1)}, u32[]{:S(2)}) copy-start(pred[12288]{0:T(1024)(128)(4,1)} %constant.329) | copy-start | bytes 36868
  10.2 51.5 %copy-start.21 = (pred[12288]{0:T(1024)(128)(4,1)S(1)}, pred[12288]{0:T(1024)(128)(4,1)}, u32[]{:S(2)}) copy-start(pred[12288]{0:T(1024)(128)(4,1)} %constant.330) | copy-start | bytes 36868
  10.2 51.5 %copy-start.22 = (pred[12288]{0:T(1024)(128)(4,1)S(1)}, pred[12288]{0:T(1024)(128)(4,1)}, u32[]{:S(2)}) copy-start(pred[12288]{0:T(1024)(128)(4,1)} %constant.331) | copy-start | bytes 36868
  10.2 51.5 %copy-start.23 = (pred[12288]{0:T(1024)(128)(4,1)S(1)}, pred[12288]{0:T(1024)(128)(4,1)}, u32[]{:S(2)}) copy-start(pred[12288]{0:T(1024)(128)(4,1)} %constant.332) | copy-start | bytes 36868
  10.2 51.5 %copy-start.24 = (pred[12288]{0:T(1024)(128)(4,1)S(1)}, pred[12288]{0:T(1024)(128)(4,1)}, u32[]{:S(2)}) copy-start(pred[12288]{0:T(1024)(128)(4,1)} %constant.333) | copy-start | bytes 36868
  10.2 51.5 %copy-start.25 = (pred[12288]{0:T(1024)(128)(4,1)S(1)}, pred[12288]{0:T(1024)(128)(4,1)}, u32[]{:S(2)}) copy-start(pred[12288]{0:T(1024)(128)(4,1)} %constant.334) | copy-start | bytes 36868
  10.2 51.5 %copy-start.26 = (pred[12288]{0:T(1024)(128)(4,1)S(1)}, pred[12288]{0:T(1024)(128)(4,1)}, u32[]{:S(2)}) copy-start(pred[12288]{0:T(1024)(128)(4,1)} %constant.335) | copy-start | bytes 36868
  10.2 51.5 %copy-start.27 = (pred[12288]{0:T(1024)(128)(4,1)S(1)}, pred[12288]{0:T(1024)(128)(4,1)}, u32[]{:S(2)}) copy-start(pred[12288]{0:T(1024)(128)(4,1)} %constant.336) | copy-start | bytes 36868
  10.2 51.5 %copy-start.28 = (pred[12288]{0:T(1024)(128)(4,1)S(1)}, pred[12288]{0:T(1024)(128)(4,1)}, u32[]{:S(2)}) copy-start(pred[12288]{0:T(1024)(128)(4,1)} %constant.337) | copy-start | bytes 36868
  10.3 51.5 %copy-start.29 = (pred[12288]{0:T(1024)(128)(4,1)S(1)}, pred[12288]{0:T(1024)(128)(4,1)}, u32[]{:S(2)}) copy-start(pred[12288]{0:T(1024)(128)(4,1)} %constant.338) | copy-start | bytes 36868
  10.3 51.5 %copy-start.30 = (pred[12288]{0:T(1024)(128)(4,1)S(1)}, pred[12288]{0:T(1024)(128)(4,1)}, u32[]{:S(2)}) copy-start(pred[12288]{0:T(1024)(128)(4,1)} %constant.339) | copy-start | bytes 36868
  10.3 51.5 %copy-start.31 = (pred[12288]{0:T(1024)(128)(4,1)S(1)}, pred[12288]{0:T(1024)(128)(4,1)}, u32[]{:S(2)}) copy-start(pred[12288]{0:T(1024)(128)(4,1)} %constant.340) | copy-start | bytes 36868
  10.3 51.5 %copy-start.32 = (pred[12288]{0:T(1024)(128)(4,1)S(1)}, pred[12288]{0:T(1024)(128)(4,1)}, u32[]{:S(2)}) copy-start(pred[12288]{0:T(1024)(128)(4,1)} %constant.341) | copy-start | bytes 36868
  221.4 63.1 %all-to-all-start = ((f32[128,8,1024]{2,1,0:T(8,128)}), f32[128,8,1024]{2,1,0:T(8,128)}, u32[]{:S(2)}, u32[]{:S(2)}) async-start(f32[128,8,1024]{2,1,0:T(8,128)} %bitcast.135), calls=%async_computation | async-start | bytes 8388608 | tf_op jit(solution)/shard_map/all_to_all | solution.py:96
  233.1 114.9 %all-reduce.8.cloned.1.call-start = ((), (), s32[]{:S(2)}) async-start(), calls=%async_computation.1 | async-start | bytes 524288 | tf_op jit(solution)/shard_map/psum | solution.py:29
  291.2 206.3 %all-reduce.10.cloned.1.call-start = ((), (), s32[]{:S(2)}) async-start(), calls=%async_computation.2 | async-start | bytes 1048576 | tf_op jit(solution)/shard_map/psum | solution.py:17
  412.5 151.0 %all-reduce.12.cloned.1.call-start = ((), (), s32[]{:S(2)}) async-start(), calls=%async_computation.3 | async-start | bytes 2097152 | tf_op jit(solution)/shard_map/psum | solution.py:36
  497.5 66.0 %copy-start.3 = (f32[256,512]{1,0:T(8,128)S(1)}, f32[256,512]{1,0:T(8,128)}, u32[]{:S(2)}) copy-start(f32[256,512]{1,0:T(8,128)} %all-reduce.10.cloned.1.call-done) | copy-start | bytes 1572868
  501.6 128.0 %all-reduce.14.cloned.1.call-start = ((), (), s32[]{:S(2)}) async-start(), calls=%async_computation.4 | async-start | bytes 524288 | tf_op jit(solution)/shard_map/psum | solution.py:29
  569.8 210.8 %all-reduce.16.cloned.1.call-start = ((), (), s32[]{:S(2)}) async-start(), calls=%async_computation.5 | async-start | bytes 1048576 | tf_op jit(solution)/shard_map/psum | solution.py:17
  668.0 112.6 %copy-start.2 = (f32[512,1024]{1,0:T(8,128)S(1)}, f32[512,1024]{1,0:T(8,128)}, u32[]{:S(2)}) copy-start(f32[512,1024]{1,0:T(8,128)} %copy-done.1) | copy-start | bytes 6291460
  695.5 151.1 %all-reduce.18.cloned.1.call-start = ((), (), s32[]{:S(2)}) async-start(), calls=%async_computation.6 | async-start | bytes 2097152 | tf_op jit(solution)/shard_map/psum | solution.py:36
  (23 other events, 845.0 us)
Sparse Core Ops, SparseCore 0:
  291.4 56.5 all-reduce.7
  412.7 84.8 all-reduce.9
  501.7 61.8 all-reduce.11
  569.9 59.5 all-reduce.13
  695.6 84.9 all-reduce.15
  784.7 61.8 all-reduce.17
where the time goes:
time: 869 us; the launch traced here: 860 us
  waiting for transfers between devices  440 us (51%)
  local copies, waits for them, and re-layouts  200 us (23%)
  other arithmetic  157 us (18%)
  matrix products  32.5 us (4%)
  between operations  17.8 us (2%)
  starting transfers between devices  12.4 us (1%)
    psum x2, waiting for transfers between devices, from_root(): return lax.psum(kept, axis)  170 us
    psum x2, waiting for transfers between devices, factor_panel(): factor = lax.psum(partial_rows, 'rt')  123 us
    psum x2, waiting for transfers between devices, factor_panel(): gram_matrix = lax.psum(gram_matrix, 'rt')  115 us
    another operation x14, other arithmetic, factor_panel(): lower_factor = jnp.linalg.cholesky(gram_matrix)  69.2 us
    gather x1, local copies, waits for them, and re-layouts, shards(): placed_cols = jnp.where(present[:, None], masked_rows.T[column_slot], 0.0)  57.3 us
    scatter x1, local copies, waits for them, and re-layouts, shards(): present = jnp.zeros((FRONT_COLS,), jnp.bool_).at[child_map].set(True)  51.6 us
    scatter x1, local copies, waits for them, and re-layouts, shards(): column_slot = jnp.zeros((FRONT_COLS,), jnp.int32).at[child_map].set(jnp.a...  45.4 us
    another operation x5, other arithmetic, factor_panel(): jax.scipy.linalg.solve_triangular(lower_factor, panel_cols.T, lower=True)  40.2 us
  transfers between devices with their start and end apart: 7, of which 7 were waited for; matrix products, arithmetic and copies ran while one was open for 2% of the time, Pallas kernels for 0%

commit v1 on v0

v1 whole, which is shorter than its diff:
```python
import functools

import jax
import jax.numpy as jnp
from jax import lax
from jax.experimental import pallas as pl
from jax.experimental.pallas import tpu as pltpu
from jax.sharding import PartitionSpec as P

TILE = 256
PANEL = 512
LANES = 128
NR = 8
NC = 16
SRC = 32
CAP = 8
ROWS_DEV = 512
BLOCK_COLS = 1024
FRONT_COLS = NC * BLOCK_COLS
FRONT_BLOCKS = FRONT_COLS // LANES

highest = lax.Precision.HIGHEST
high = lax.Precision.HIGH
f32 = jnp.float32
bf16 = jnp.bfloat16
MESH = pl.DeviceIdType.MESH


def place_kernel(q_ref, lim_ref, ch_ref, code_ref, sel_ref, out_ref, panel_ref):
    step = pl.program_id(0)
    row_ids = lax.broadcasted_iota(jnp.int32, (SRC, LANES), 0)
    sel = sel_ref[...]
    per_step = BLOCK_COLS // LANES
    for sub in range(per_step):
        b = step * per_step + sub
        q = q_ref[b]
        start = pl.multiple_of(q * LANES, LANES)
        v0 = ch_ref[:, pl.ds(start, LANES)]
        v1 = ch_ref[:, pl.ds(pl.multiple_of(start + LANES, LANES), LANES)]
        v0 = jnp.where(row_ids < lim_ref[q], v0, 0.0)
        v1 = jnp.where(row_ids < lim_ref[q + 1], v1, 0.0)
        code = jnp.broadcast_to(code_ref[pl.ds(b, 1), :], (SRC, LANES))
        lane = jnp.bitwise_and(code, LANES - 1)
        g0 = jnp.take_along_axis(v0, lane, axis=1)
        g1 = jnp.take_along_axis(v1, lane, axis=1)
        x = jnp.where(code < 0, 0.0, jnp.where(code < LANES, g0, g1))
        hi = x.astype(bf16)
        rest = x - hi.astype(f32)
        mid = rest.astype(bf16)
        low = (rest - mid.astype(f32)).astype(bf16)
        parts = jnp.concatenate([hi, mid, low], axis=0)
        y = jnp.dot(sel, parts, preferred_element_type=f32)
        y = y.reshape(NR, CAP, LANES)
        out_ref[:, 0, :, sub * LANES : (sub + 1) * LANES] = y
        if sub < PANEL // LANES:

            @pl.when(step == 0)
            def _():
                panel_ref[:, :, sub * LANES : (sub + 1) * LANES] = y


def place(children, code, q, lim, sel):
    child_cols = children.shape[1]
    return pl.pallas_call(
        place_kernel,
        grid_spec=pltpu.PrefetchScalarGridSpec(
            num_scalar_prefetch=2,
            grid=(NC,),
            in_specs=[
                pl.BlockSpec((SRC, child_cols), lambda i, *_: (0, 0)),
                pl.BlockSpec((FRONT_BLOCKS, LANES), lambda i, *_: (0, 0)),
                pl.BlockSpec((NR * CAP, 3 * SRC), lambda i, *_: (0, 0)),
            ],
            out_specs=[
                pl.BlockSpec((NR, 1, CAP, BLOCK_COLS), lambda i, *_: (0, i, 0, 0)),
                pl.BlockSpec((NR, CAP, PANEL), lambda i, *_: (0, 0, 0)),
            ],
        ),
        out_shape=[
            jax.ShapeDtypeStruct((NR, NC, CAP, BLOCK_COLS), f32),
            jax.ShapeDtypeStruct((NR, CAP, PANEL), f32),
        ],
        cost_estimate=pl.CostEstimate(flops=400_000_000, bytes_accessed=6_000_000, transcendentals=0),
    )(q, lim, children, code, sel)


def panel_kernel(
    po_ref, a_ref, g_ref, chunk, abuf, gpart, gin, gsum, gbuf, s1, r1, s2, r2, s3, r3, s4, r4
):
    r = lax.axis_index("rt")
    c = lax.axis_index("ct")
    barrier = pltpu.get_barrier_semaphore()
    for d in range(1, NR):
        pl.semaphore_signal(barrier, inc=1, device_id=(lax.rem(r + d, NR), c), device_id_type=MESH)
    for e in range(1, NC):
        pl.semaphore_signal(barrier, inc=1, device_id=(r, lax.rem(c + e, NC)), device_id_type=MESH)
    pl.semaphore_wait(barrier, NR + NC - 2)

    def to_rt(src_of, dst, send, recv):
        copies = []
        for d in range(1, NR):
            t = lax.rem(r + d, NR)
            copy = pltpu.make_async_remote_copy(
                src_ref=src_of(t),
                dst_ref=dst,
                send_sem=send.at[d - 1],
                recv_sem=recv.at[d - 1],
                device_id=(t, c),
                device_id_type=MESH,
            )
            copy.start()
            copies.append(copy)
        return copies

    def to_ct(src, dst, send, recv):
        copies = []
        for e in range(1, NC):
            copy = pltpu.make_async_remote_copy(
                src_ref=src,
                dst_ref=dst,
                send_sem=send.at[e - 1],
                recv_sem=recv.at[e - 1],
                device_id=(r, lax.rem(c + e, NC)),
                device_id_type=MESH,
            )
            copy.start()
            copies.append(copy)
        return copies

    copies = to_rt(lambda t: po_ref.at[t], chunk.at[r], s1, r1)
    chunk[r] = po_ref[r]
    for copy in copies:
        copy.wait()
    copies = to_ct(chunk, abuf.at[:, c], s2, r2)
    abuf[:, c] = chunk[...]
    for copy in copies:
        copy.wait()
    whole = abuf[...].reshape(NR * NC * CAP, PANEL)
    a_ref[...] = whole

    def gram_rows(i, carry):
        cols = a_ref[:, pl.ds(pl.multiple_of(i * LANES, LANES), LANES)]
        rows = lax.dot_general(
            cols.T, a_ref[...], (((1,), (0,)), ((), ())), precision=highest, preferred_element_type=f32
        )
        per = LANES // SRC
        gpart[pl.ds(i * per, per)] = rows.reshape(per, SRC, PANEL)
        return carry

    lax.fori_loop(0, PANEL // LANES, gram_rows, 0)
    copies = to_rt(lambda t: gpart.at[c], gin.at[r], s3, r3)
    gin[r] = gpart[c]
    for copy in copies:
        copy.wait()
    total = gin[0]
    for t in range(1, NR):
        total = total + gin[t]
    gsum[...] = total
    copies = to_ct(gsum, gbuf.at[c], s4, r4)
    gbuf[c] = total
    for copy in copies:
        copy.wait()
    g_ref[...] = gbuf[...].reshape(PANEL, PANEL)


def gather_panel(panel_out):
    slots = NR * NC * CAP
    dma = pltpu.SemaphoreType.DMA
    return pl.pallas_call(
        panel_kernel,
        in_specs=[pl.BlockSpec(memory_space=pltpu.VMEM)],
        out_specs=[pl.BlockSpec(memory_space=pltpu.VMEM)] * 2,
        out_shape=[
            jax.ShapeDtypeStruct((slots, PANEL), f32),
            jax.ShapeDtypeStruct((PANEL, PANEL), f32),
        ],
        scratch_shapes=[
            pltpu.VMEM((NR, CAP, PANEL), f32),
            pltpu.VMEM((NR, NC, CAP, PANEL), f32),
            pltpu.VMEM((NC, SRC, PANEL), f32),
            pltpu.VMEM((NR, SRC, PANEL), f32),
            pltpu.VMEM((SRC, PANEL), f32),
            pltpu.VMEM((NC, SRC, PANEL), f32),
            dma((NR - 1,)),
            dma((NR - 1,)),
            dma((NC - 1,)),
            dma((NC - 1,)),
            dma((NR - 1,)),
            dma((NR - 1,)),
            dma((NC - 1,)),
            dma((NC - 1,)),
        ],
        compiler_params=pltpu.CompilerParams(collective_id=0, has_side_effects=True),
        cost_estimate=pl.CostEstimate(flops=600_000_000, bytes_accessed=100_000_000, transcendentals=0),
    )(panel_out)


def sum_kernel(p_ref, out_ref, ain, half, bin_ref, mine, full, sa, ra, sb, rb, sc, rc, sd, rd):
    r = lax.axis_index("rt")
    c = lax.axis_index("ct")
    core = lax.rem(r, 2)
    x = r // 2
    sibling = r + 1 - 2 * core
    chips = NR // 2
    barrier = pltpu.get_barrier_semaphore()
    pl.semaphore_signal(barrier, inc=1, device_id=(sibling, c), device_id_type=MESH)
    peers = [2 * lax.rem(x + d, chips) + core for d in range(1, chips)]
    for peer in peers:
        pl.semaphore_signal(barrier, inc=1, device_id=(peer, c), device_id_type=MESH)
    pl.semaphore_wait(barrier, chips)

    def send(src, dst, ss, rs, to):
        copy = pltpu.make_async_remote_copy(
            src_ref=src, dst_ref=dst, send_sem=ss, recv_sem=rs, device_id=(to, c), device_id_type=MESH
        )
        copy.start()
        return copy

    swap = send(p_ref.at[1 - core], ain, sa, ra, sibling)
    swap.wait()
    half[...] = p_ref[core] + ain[...]
    copies = [
        send(half.at[peer // 2], bin_ref.at[d], sb.at[d], rb.at[d], peer)
        for d, peer in enumerate(peers)
    ]
    for copy in copies:
        copy.wait()
    mine[...] = (half[x] + bin_ref[0]) + (bin_ref[1] + bin_ref[2])
    copies = [
        send(mine, full.at[core, x], sc.at[d], rc.at[d], peer) for d, peer in enumerate(peers)
    ]
    last = [send(mine, full.at[core, x], sd.at[chips - 1], rd.at[chips - 1], sibling)]
    full[core, x] = mine[...]
    for d, copy in enumerate(copies):
        copy.wait()
        owner = lax.rem(x + chips - d - 1, chips)
        last.append(
            send(full.at[core, owner], full.at[core, owner], sd.at[d], rd.at[d], sibling)
        )
    for copy in last:
        copy.wait()
    out_ref[...] = full[...].reshape(out_ref.shape)


def sum_over_rt(part):
    rows, cols = part.shape
    chips = NR // 2
    sl = rows // NR
    dma = pltpu.SemaphoreType.DMA
    return pl.pallas_call(
        sum_kernel,
        in_specs=[pl.BlockSpec(memory_space=pltpu.VMEM)],
        out_specs=pl.BlockSpec(memory_space=pltpu.VMEM),
        out_shape=jax.ShapeDtypeStruct((rows, cols), f32),
        scratch_shapes=[
            pltpu.VMEM((chips, sl, cols), f32),
            pltpu.VMEM((chips, sl, cols), f32),
            pltpu.VMEM((chips - 1, sl, cols), f32),
            pltpu.VMEM((sl, cols), f32),
            pltpu.VMEM((2, chips, sl, cols), f32),
            dma(()),
            dma(()),
            dma((chips - 1,)),
            dma((chips - 1,)),
            dma((chips - 1,)),
            dma((chips - 1,)),
            dma((chips,)),
            dma((chips,)),
        ],
        compiler_params=pltpu.CompilerParams(collective_id=1, has_side_effects=True),
        cost_estimate=pl.CostEstimate(flops=1_000_000, bytes_accessed=100_000_000, transcendentals=0),
    )(part.reshape(2, chips, sl, cols))


def tables(row_map, column_map, staircase, r, c):
    sources = NR * NC
    device_id = r * NC + c
    which_child = r // (NR // 2)
    tile = (row_map // ROWS_DEV).reshape(sources, SRC)
    same = tile[:, :, None] == tile[:, None, :]
    before = jnp.arange(SRC)[:, None] > jnp.arange(SRC)[None, :]
    rank = jnp.sum((same & before[None]).astype(jnp.int32), axis=2)
    my_slot = lax.dynamic_index_in_dim(tile * CAP + rank, device_id, 0, keepdims=False)
    select = my_slot[None, :] == jnp.arange(NR * CAP, dtype=jnp.int32)[:, None]
    select = jnp.tile(select.astype(bf16), (1, 3))
    local = row_map.reshape(sources, SRC) - r * ROWS_DEV
    hit = (tile == r)[:, :, None] & (rank[:, :, None] == jnp.arange(CAP)[None, None, :])
    front_of_slot = jnp.sum(jnp.where(hit, local[:, :, None] + 1, 0), axis=1).reshape(-1) - 1
    slot_of_front = jnp.sum(
        jnp.where(
            front_of_slot[None, :] == jnp.arange(ROWS_DEV, dtype=jnp.int32)[:, None],
            jnp.arange(sources * CAP, dtype=jnp.int32)[None, :],
            0,
        ),
        axis=1,
    )
    cmap = lax.dynamic_index_in_dim(column_map, which_child, 0, keepdims=False)
    stair = lax.dynamic_index_in_dim(staircase, which_child, 0, keepdims=False)
    blocks = jnp.arange(FRONT_BLOCKS, dtype=jnp.int32)
    high_part = ((cmap // LANES)[None, :] == blocks[:, None]).astype(bf16)
    low_part = ((cmap % LANES)[None, :] == jnp.arange(LANES, dtype=jnp.int32)[:, None]).astype(bf16)
    present = lax.dot_general(high_part, low_part, (((1,), (1,)), ((), ())), preferred_element_type=f32)
    upper = (jnp.arange(LANES)[:, None] < jnp.arange(LANES)[None, :]).astype(bf16)
    inside = jnp.dot(present.astype(bf16), upper, preferred_element_type=f32)
    counts = jnp.sum(present, axis=1)
    starts = jnp.sum(jnp.where(blocks[None, :] < blocks[:, None], counts[None, :], 0.0), axis=1)
    starts = starts.astype(jnp.int32)
    child_blocks = cmap.shape[0] // LANES
    q = jnp.minimum(starts // LANES, child_blocks - 2)
    code = starts[:, None] + inside.astype(jnp.int32) - q[:, None] * LANES
    code = jnp.where(present > 0.5, code, -1)
    first = lax.rem(device_id * SRC, row_map.shape[0] // 2)
    lim = jnp.repeat(stair, TILE // LANES, total_repeat_length=child_blocks) - first
    return select, slot_of_front, code, q, lim


def shards(children, row_map, column_map, staircase):
    r = lax.axis_index("rt")
    c = lax.axis_index("ct")
    select, slot_of_front, code, q, lim = tables(row_map, column_map, staircase, r, c)
    outgoing, panel_out = place(children, code, q, lim, select)
    arrived = lax.all_to_all(
        outgoing.reshape(NR * NC, CAP, BLOCK_COLS),
        ("rt", "ct"),
        split_axis=0,
        concat_axis=0,
        tiled=True,
    )
    panel_rows, gram = gather_panel(panel_out)
    lower = jnp.linalg.cholesky(gram)
    inverse = jax.scipy.linalg.solve_triangular(lower, jnp.eye(PANEL, dtype=f32), lower=True)
    arrived = arrived.reshape(NR * NC * CAP, BLOCK_COLS)
    part = lax.dot_general(
        panel_rows, arrived, (((0,), (0,)), ((), ())), precision=high, preferred_element_type=f32
    )
    projected = sum_over_rt(part)
    front_block = arrived[slot_of_front]
    panel_block = panel_rows[slot_of_front]
    basis = lax.dot_general(
        inverse, panel_block, (((1,), (1,)), ((), ())), precision=high, preferred_element_type=f32
    )
    factor_rows = jnp.dot(inverse, projected, precision=high, preferred_element_type=f32)
    update = lax.dot_general(
        basis, factor_rows, (((0,), (0,)), ((), ())), precision=high, preferred_element_type=f32
    )
    return (factor_rows, basis, front_block - update)


def solution(mesh):
    placed = (P(("rt", "ct"), None), P(), P(), P())
    return jax.shard_map(
        shards,
        mesh=mesh,
        in_specs=placed,
        out_specs=(P(None, "ct"), P(None, "rt"), P("rt", "ct")),
        check_vma=False,
    )
```

time: 869 us -> 379 us (0.44)
  waiting for transfers between devices: 440 us -> 0.01 us
  Pallas kernels: 0 us -> 172 us
  local copies, waits for them, and re-layouts: 200 us -> 29.1 us
  other arithmetic: 157 us -> 124 us
  between operations: 17.8 us -> 3.84 us
    psum x6 -> x0, waiting for transfers between devices: 407 us -> none  [the longest x2 170 us: from_root(): return lax.psum(kept, axis)]
    pallas_call x0 -> x3, Pallas kernels: none -> 172 us  [the longest x1 113 us: gather_panel(): pl.pallas_call(panel_kernel, in_specs=[pl.BlockSpec(memory_space=pltpu.VM...]
    scatter x3 -> x0, local copies, waits for them, and re-layouts: 113 us -> none  [the longest x1 51.6 us: shards(): present = jnp.zeros((FRONT_COLS,), jnp.bool_).at[child_map].set(True)]
    gather x6 -> x3, local copies, waits for them, and re-layouts: 67.5 us -> 8.65 us  [the longest x1 5.09 us: shards(): front_block = arrived[slot_of_front]]
    all_to_all x1, waiting for transfers between devices: 32.3 us -> 0.01 us  [shards(): lax.all_to_all(outgoing.reshape(NR * NC, CAP, BLOCK_COLS), ('rt', 'ct'),...]
    gather x4 -> x2, other arithmetic: 31.1 us -> 0.01 us  [the longest x1 0.01 us: tables(): jnp.repeat(stair, TILE // LANES, total_repeat_length=child_blocks) - first]
    another operation x20 -> x17, other arithmetic: 109 us -> 120 us  [the longest x14 78.7 us: shards(): lower = jnp.linalg.cholesky(gram)]
    transpose x1 -> x0, other arithmetic: 9.83 us -> none  [shards(): placed_cols = jnp.where(present[:, None], masked_rows.T[column_slot], 0.0)]
  transfers between devices with their start and end apart: 7 -> 1, of which waited for: 7 -> 0; matrix products, arithmetic and copies ran while one was open for 2% -> 42% of each run, Pallas kernels for 0% -> 30%
where the time goes in v1:
time: 379 us; the launch traced here: 372 us
  Pallas kernels  172 us (45%)
  other arithmetic  124 us (33%)
  matrix products  32.5 us (9%)
  local copies, waits for them, and re-layouts  29.1 us (8%)
  starting transfers between devices  11.7 us (3%)
  between operations  3.84 us (1%)
    pallas_call x1, Pallas kernels, gather_panel(): pl.pallas_call(panel_kernel, in_specs=[pl.BlockSpec(memory_space=pltpu.VM...  113 us
    another operation x14, other arithmetic, shards(): lower = jnp.linalg.cholesky(gram)  78.7 us
    another operation x3, other arithmetic, shards(): jax.scipy.linalg.solve_triangular(lower, jnp.eye(PANEL, dtype=f32), lower...  41.2 us
    pallas_call x1, Pallas kernels, sum_over_rt(): pl.pallas_call(sum_kernel, in_specs=[pl.BlockSpec(memory_space=pltpu.VMEM...  37.3 us
    pallas_call x1, Pallas kernels, place(): pl.pallas_call(place_kernel, grid_spec=pltpu.PrefetchScalarGridSpec(num_s...  20.9 us
    another operation x12, local copies, waits for them, and re-layouts  14.3 us
    all_to_all x1, starting transfers between devices, shards(): lax.all_to_all(outgoing.reshape(NR * NC, CAP, BLOCK_COLS), ('rt', 'ct'),...  11.7 us
  transfers between devices with their start and end apart: 1, of which 0 were waited for; matrix products, arithmetic and copies ran while one was open for 42% of the time, Pallas kernels for 30%

profile of v1, /device:TPU:0, one launch (start us, length us, event | category | flops | bytes accessed | tf_op | source)
XLA Modules:
  0.0 372.5 jit_solution(18153699598890316094)
XLA Ops:
  1.9 1.9 fusion.53
  8.5 20.9 %shard_map.67 = (f32[8,16,8,1024]{3,2,1,0:T(8,128)}, f32[8,8,512]{2,1,0:T(8,128)}) custom-call(s32[128]{0:T(128)} %get-tuple-element.40.q_ref, s32[96]{0:T(128)} %broadcast_subtract_fusion.lim_ref, f32[32,12288]{1,0:T(8,128)} %ch_ref.1, s32[128,128]{1,0:T(8,128)} %fusion.7.code_ref, bf16[64,96]{1,0:T(8,128)(2,1)} %copy.27.sel_ref), custom_call_target="tpu_custom_call" | custom-call | flops 400000000 | bytes 6000000 | tf_op jit(solution)/shard_map/pallas_call | solution.py:64
  29.4 11.7 %all-to-all-start = ((f32[128,8,1024]{2,1,0:T(8,128)}), f32[128,8,1024]{2,1,0:T(8,128)}, u32[]{:S(2)}, u32[]{:S(2)}) async-start(f32[128,8,1024]{2,1,0:T(8,128)} %bitcast.72), calls=%async_computation | async-start | bytes 8388608 | tf_op jit(solution)/shard_map/all_to_all | solution.py:322
  41.2 113.4 %shard_map.68 = (f32[1024,512]{1,0:T(8,128)}, f32[512,512]{1,0:T(8,128)}) custom-call(f32[8,8,512]{2,1,0:T(8,128)} %get-tuple-element.19.po_ref), custom_call_target="tpu_custom_call" | custom-call | flops 600000000 | bytes 100000000 | tf_op jit(solution)/shard_map/pallas_call | solution.py:169
  154.6 1.6 copy.28
  157.5 11.7 %cholesky.103 = f32[128,128]{1,0:T(8,128)S(1)} custom-call(f32[128,128]{1,0:T(8,128)S(1)} %cholesky.263), custom_call_target="Cholesky" | custom-call | tf_op jit(solution)/shard_map/jit(cholesky)/cholesky | solution.py:330
  169.4 9.8 %custom-call.31 = f32[1,128,128]{1,2,0:T(8,128)S(1)} custom-call(f32[1,128,128]{2,1,0:T(8,128)S(1)} %get-tuple-element.54), custom_call_target="InvertDiagBlocksLowerTriangular" | custom-call | tf_op jit(solution)/shard_map/jit(cholesky)/cholesky | solution.py:330
  179.2 1.2 constant_dynamic-update-slice_fusion
  180.4 1.3 convolution_subtract_fusion.4
  181.7 11.7 %cholesky.214 = f32[128,128]{1,0:T(8,128)S(1)} custom-call(f32[128,128]{1,0:T(8,128)S(1)} %cholesky.267), custom_call_target="Cholesky" | custom-call | tf_op jit(solution)/shard_map/jit(cholesky)/cholesky | solution.py:330
  193.5 10.2 %custom-call.32 = f32[1,128,128]{1,2,0:T(8,128)S(1)} custom-call(f32[1,128,128]{2,1,0:T(8,128)S(1)} %get-tuple-element.51), custom_call_target="InvertDiagBlocksLowerTriangular" | custom-call | tf_op jit(solution)/shard_map/jit(cholesky)/cholesky | solution.py:330
  203.9 1.3 convolution_subtract_fusion.5
  205.2 11.7 %cholesky.235 = f32[128,128]{1,0:T(8,128)S(1)} custom-call(f32[128,128]{1,0:T(8,128)S(1)} %cholesky.272), custom_call_target="Cholesky" | custom-call | tf_op jit(solution)/shard_map/jit(cholesky)/cholesky | solution.py:330
  217.7 9.8 %custom-call.33 = f32[1,128,128]{1,2,0:T(8,128)S(1)} custom-call(f32[1,128,128]{2,1,0:T(8,128)S(1)} %get-tuple-element.48), custom_call_target="InvertDiagBlocksLowerTriangular" | custom-call | tf_op jit(solution)/shard_map/jit(cholesky)/cholesky | solution.py:330
  227.7 1.2 convolution_subtract_fusion.6
  228.9 11.7 %cholesky.252 = f32[128,128]{1,0:T(8,128)S(1)} custom-call(f32[128,128]{1,0:T(8,128)S(1)} %convolution_subtract_fusion.6), custom_call_target="Cholesky" | custom-call | tf_op jit(solution)/shard_map/jit(cholesky)/cholesky | solution.py:330
  245.5 14.3 %while.2 = (s32[]{:T(128)}, f32[512,512]{1,0:T(8,128)}, s32[4,2]{0,1:T(2,128)S(1)}, f32[4,128,128]{2,1,0:T(8,128)}, s32[]{:T(128)}) while((s32[]{:T(128)}, f32[512,512]{1,0:T(8,128)}, s32[4,2]{0,1:T(2,128)S(1)}, f32[4,128,128]{2,1,0:T(8,128)}, s32[]{:T(128)}) %tuple.39), condition=%wide.while_cond.1, body=%wide.while_body.1.sunk | while | flops 2 | bytes 132705 | solution.py:331
  246.2 2.9 bitcast_dynamic-update-slice_fusion.2
  249.8 2.9 bitcast_dynamic-update-slice_fusion.2
  253.4 2.9 bitcast_dynamic-update-slice_fusion.2
  257.0 2.9 bitcast_dynamic-update-slice_fusion.2
  259.9 40.1 %custom-call.34 = f32[4,128,128]{1,2,0:T(8,128)S(1)} custom-call(f32[4,128,128]{2,1,0:T(8,128)} %get-tuple-element.30), custom_call_target="InvertDiagBlocksLowerTriangular" | custom-call | tf_op jit(solution)/shard_map/jit(_solve_triangular)/triangular_solve | solution.py:331
  300.8 2.3 gather_fusion.1
  303.2 2.0 copy.29
  307.3 1.3 convolution_subtract_fusion.1
  309.1 1.6 convolution_subtract_fusion.3
  311.1 2.0 fusion.14
  313.1 7.0 %fusion.1.p_ref = f32[2,4,64,1024]{3,2,1,0:T(8,128)} fusion(f32[2,4,64,1024]{3,2,1,0:T(8,128)S(1)} %bitcast.71, f32[128,8,1024]{2,1,0:T(8,128)} %all-to-all-done), kind=kOutput, calls=%fused_computation.8 | convolution fusion | flops 3221225472 | bytes 8388608 | tf_op jit(solution)/shard_map/dot_general | solution.py:333
  320.2 37.3 %shard_map.69 = f32[512,1024]{1,0:T(8,128)} custom-call(f32[2,4,64,1024]{3,2,1,0:T(8,128)} %fusion.1.p_ref), custom_call_target="tpu_custom_call" | custom-call | flops 1000000 | bytes 100000000 | tf_op jit(solution)/shard_map/pallas_call | solution.py:250
  357.5 4.8 %fusion.15 = f32[512,1024]{1,0:T(8,128)} fusion(f32[512,1024]{1,0:T(8,128)} %shard_map.69, f32[128,512]{1,0:T(8,128)S(1)} %fusion.31, f32[128,512]{1,0:T(8,128)S(1)} %fusion.32, f32[128,512]{1,0:T(8,128)S(1)} %fusion.34, f32[128,512]{1,0:T(8,128)S(1)} %fusion.21), kind=kOutput, calls=%fused_computation.39 | convolution fusion | flops 1611399168 | bytes 5242880 | tf_op jit(solution)/shard_map/dot_general | solution.py:342
  362.3 5.1 %gather_fusion.2 = f32[512,1024]{1,0:T(8,128)S(1)} fusion(f32[1024,1024]{1,0:T(8,128)} %bitcast.18, s32[1024]{0:T(1024)S(1)} %pad_clamp_fusion), kind=kCustom, calls=%fused_computation.2 | custom fusion | bytes 4196352 | tf_op jit(solution)/shard_map/gather | solution.py:337
  367.4 4.9 %convolution_subtract_fusion = f32[512,1024]{1,0:T(8,128)} fusion(f32[512,1024]{1,0:T(8,128)S(1)} %gather_fusion.2, f32[512,512]{1,0:T(8,128)S(1)} %copy-done.3, f32[512,1024]{1,0:T(8,128)} %fusion.15), kind=kOutput, calls=%fused_computation.14 | convolution fusion | flops 1611137024 | bytes 7340032 | tf_op jit(solution)/shard_map/dot_general | solution.py:343
  (83 shorter events, 17.3 us)
Async XLA Ops:
  0.6 3.9 %copy-start = (s32[2,48]{1,0:T(2,128)S(1)}, s32[2,48]{1,0:T(2,128)}, u32[]{:S(2)}) copy-start(s32[2,48]{1,0:T(2,128)} %param.9) | copy-start | bytes 1156
  1.9 2.6 copy-start.8
  1.9 2.7 copy-start.7
  29.4 283.7 %all-to-all-start = ((f32[128,8,1024]{2,1,0:T(8,128)}), f32[128,8,1024]{2,1,0:T(8,128)}, u32[]{:S(2)}, u32[]{:S(2)}) async-start(f32[128,8,1024]{2,1,0:T(8,128)} %bitcast.72), calls=%async_computation | async-start | bytes 8388608 | tf_op jit(solution)/shard_map/all_to_all | solution.py:322
  154.6 1.7 copy-start.5
  156.5 1.0 copy-start.6
  217.0 83.9 %copy-start.1 = (f32[1024,512]{1,0:T(8,128)S(1)}, f32[1024,512]{1,0:T(8,128)}, u32[]{:S(2)}) copy-start(f32[1024,512]{1,0:T(8,128)} %get-tuple-element.21) | copy-start | bytes 6291460
  306.9 4.2 %copy-start.4 = (f32[512,512]{1,0:T(8,128)S(1)}, f32[512,512]{1,0:T(8,128)}, u32[]{:S(2)}) copy-start(f32[512,512]{1,0:T(8,128)} %gather_fusion.1) | copy-start | bytes 3145732
  310.7 2.5 copy-start.2
  362.3 5.1 %copy-start.3 = (f32[512,512]{1,0:T(8,128)S(1)}, f32[512,512]{1,0:T(8,128)}, u32[]{:S(2)}) copy-start(f32[512,512]{1,0:T(8,128)} %fusion.14) | copy-start | bytes 3145732

commit v2 on v1

v2 whole, which is shorter than its diff:
```python
import functools

import jax
import jax.numpy as jnp
from jax import lax
from jax.experimental import pallas as pl
from jax.experimental.pallas import tpu as pltpu
from jax.sharding import PartitionSpec as P

TILE = 256
PANEL = 512
SUB = 8
LANES = 128
NR = 8
NC = 16
SRC = 32
CAP = 8
ROWS_DEV = 512
BLOCK_COLS = 1024
FRONT_COLS = NC * BLOCK_COLS
FRONT_BLOCKS = FRONT_COLS // LANES
QUARTERS = 4
QCOLS = BLOCK_COLS // QUARTERS
SIDE = 4
CHIPS = NR // 2
SLICE = PANEL // NR
PAIRS = [(i, j) for i in range(PANEL // LANES) for j in range(i, PANEL // LANES)]

highest = lax.Precision.HIGHEST
high = lax.Precision.HIGH
f32 = jnp.float32
bf16 = jnp.bfloat16
MESH = pl.DeviceIdType.MESH


def place_kernel(q_ref, lim_ref, ch_ref, code_ref, out_ref, panel_ref):
    step = pl.program_id(0)
    row_ids = lax.broadcasted_iota(jnp.int32, (SUB, LANES), 0)
    per_step = BLOCK_COLS // LANES
    for sub in range(per_step):
        b = step * per_step + sub
        q = q_ref[b]
        start = pl.multiple_of(q * LANES, LANES)
        after = pl.multiple_of(start + LANES, LANES)
        code = jnp.broadcast_to(code_ref[pl.ds(b, 1), :], (SUB, LANES))
        lane = jnp.bitwise_and(code, LANES - 1)
        first = lim_ref[q]
        second = lim_ref[q + 1]
        limit = jnp.where(code < LANES, first, second)
        limit = jnp.where(code < 0, 0, limit)
        quarter, offset = divmod(sub * LANES, QCOLS)
        for g in range(SRC // SUB):
            v0 = ch_ref[g * SUB : (g + 1) * SUB, pl.ds(start, LANES)]
            v1 = ch_ref[g * SUB : (g + 1) * SUB, pl.ds(after, LANES)]
            g0 = jnp.take_along_axis(v0, lane, axis=1)
            g1 = jnp.take_along_axis(v1, lane, axis=1)
            x = jnp.where(code < LANES, g0, g1)
            x = jnp.where(row_ids + g * SUB < limit, x, 0.0)
            out_ref[quarter, 0, g * SUB : (g + 1) * SUB, offset : offset + LANES] = x
            if sub < PANEL // LANES:

                @pl.when(step == 0)
                def _():
                    panel_ref[g * SUB : (g + 1) * SUB, sub * LANES : (sub + 1) * LANES] = x


def place(children, code, q, lim):
    child_cols = children.shape[1]
    return pl.pallas_call(
        place_kernel,
        grid_spec=pltpu.PrefetchScalarGridSpec(
            num_scalar_prefetch=2,
            grid=(NC,),
            in_specs=[
                pl.BlockSpec((SRC, child_cols), lambda i, *_: (0, 0)),
                pl.BlockSpec((FRONT_BLOCKS, LANES), lambda i, *_: (0, 0)),
            ],
            out_specs=[
                pl.BlockSpec((QUARTERS, 1, SRC, QCOLS), lambda i, *_: (0, i, 0, 0)),
                pl.BlockSpec((SRC, PANEL), lambda i, *_: (0, 0)),
            ],
        ),
        out_shape=[
            jax.ShapeDtypeStruct((QUARTERS, NC, SRC, QCOLS), f32),
            jax.ShapeDtypeStruct((SRC, PANEL), f32),
        ],
        cost_estimate=pl.CostEstimate(flops=10_000_000, bytes_accessed=4_000_000, transcendentals=0),
    )(q, lim, children, code)


def across_lanes(v, lane):
    return jnp.broadcast_to(v[:, lane : lane + 1], (SUB, LANES))

def across_rows(v, row):
    return jnp.broadcast_to(v[row : row + 1, :], (SUB, LANES))

def inverse_of_block(block, unit, write):
    groups = LANES // SUB
    sub = lax.broadcasted_iota(jnp.int32, (SUB, LANES), 0)
    for g in range(groups):
        cols = [across_lanes(block[g], SUB * g + m) for m in range(SUB)]
        a = {(i, m): across_rows(cols[m], i) for m in range(SUB) for i in range(m, SUB)}
        low = {}
        inv = {}
        for k in range(SUB):
            inv[k, k] = lax.rsqrt(a[k, k])
            for i in range(k + 1, SUB):
                low[i, k] = a[i, k] * inv[k, k]
            for i in range(k + 1, SUB):
                for m in range(k + 1, i + 1):
                    a[i, m] = a[i, m] - low[i, k] * low[m, k]
        for i in range(1, SUB):
            for k in range(i):
                acc = low[i, k] * inv[k, k]
                for m in range(k + 1, i):
                    acc = acc + low[i, m] * inv[m, k]
                inv[i, k] = -inv[i, i] * acc
        zero = jnp.zeros((SUB, LANES), f32)
        down = []
        for k in range(SUB):
            col = zero
            for i in range(k, SUB):
                col = jnp.where(sub == i, inv[i, k], col)
            down.append(col)
        up = []
        for k in range(SUB):
            col = zero
            for i in range(k + 1):
                col = jnp.where(sub == i, inv[k, i], col)
            up.append(col)

        def apply(cols, v):
            terms = [cols[k] * across_rows(v, k) for k in range(SUB)]
            while len(terms) > 1:
                terms = [terms[i] + terms[i + 1] for i in range(0, len(terms), 2)]
            return terms[0]

        done = apply(down, unit[g])
        write(g, done)
        if g + 1 < groups:
            z = apply(up, apply(down, block[g]))
            zu = apply(up, done)
            zr = [across_rows(z, m) for m in range(SUB)]
            zur = [across_rows(zu, m) for m in range(SUB)]
            for i in range(g + 1, groups):
                mult = [across_lanes(block[i], SUB * g + m) for m in range(SUB)]
                t = [mult[m] * zr[m] for m in range(SUB)]
                u = [mult[m] * zur[m] for m in range(SUB)]
                while len(t) > 1:
                    t = [t[j] + t[j + 1] for j in range(0, len(t), 2)]
                    u = [u[j] + u[j + 1] for j in range(0, len(u), 2)]
                block[i] = block[i] - t[0]
                unit[i] = unit[i] - u[0]


def three_parts(x):
    hi = x.astype(bf16)
    rest = x - hi.astype(f32)
    mid = rest.astype(bf16)
    low = (rest - mid.astype(f32)).astype(bf16)
    return jnp.concatenate([hi, mid, low], axis=0)


def two_parts(x):
    hi = x.astype(bf16)
    return hi, (x - hi.astype(f32)).astype(bf16)


class GatherCt:
    def __init__(self, source, dest, r, c, s1, r1, s2, r2):
        self.source, self.dest, self.r, self.c = source, dest, r, c
        self.sems = (s1, r1, s2, r2)
        self.first, self.second = [], []

    def along(self, half, d):
        z, y = self.c // SIDE, lax.rem(self.c, SIDE)
        if half == 0:
            return z * SIDE + lax.rem(y + d, SIDE)
        return lax.rem(z + d, SIDE) * SIDE + y

    def send(self, src, half, owner, to, ss, rs):
        copy = pltpu.make_async_remote_copy(
            src_ref=src,
            dst_ref=self.dest(half, owner),
            send_sem=ss,
            recv_sem=rs,
            device_id=(self.r, to),
            device_id_type=MESH,
        )
        copy.start()
        return copy

    def start(self):
        s1, r1, s2, r2 = self.sems
        for d in range(1, SIDE):
            for h in range(2):
                to = self.along(h, d)
                copy = self.send(self.source(h), h, self.c, to, s1.at[h, d - 1], r1.at[h, d - 1])
                self.first.append(copy)
        for d in range(1, SIDE):
            for h in range(2):
                to = self.along(1 - h, d)
                copy = self.send(
                    self.source(h), h, self.c, to, s2.at[h, 0, d - 1], r2.at[h, 0, d - 1]
                )
                self.second.append(copy)

    def forward(self):
        s1, r1, s2, r2 = self.sems
        position = 0
        for p in range(1, SIDE):
            for h in range(2):
                self.first[position].wait()
                position += 1
                owner = self.along(h, SIDE - p)
                for d in range(1, SIDE):
                    to = self.along(1 - h, d)
                    copy = self.send(
                        self.dest(h, owner), h, owner, to, s2.at[h, p, d - 1], r2.at[h, p, d - 1]
                    )
                    self.second.append(copy)

    def finish(self):
        for copy in self.second:
            copy.wait()


def front_kernel(
    x_ref, pan_ref, sel_ref, fs_ref, as_ref, sum_ref, inv_ref,
    po, chunk, ap, apt, gpart, gin, gsum, gbuf, fp, routed, work, small,
    part, ain, half, bin_ref, mine, full,
    p1s, p1r, a1s, a1r, a2s, a2r, c1s, c1r, c2s, c2r, g1s, g1r, g2s, g2r, p3s, p3r,
    t1s, t1r, t2s, t2r, sa, ra, sb, rb, sc, rc, sd, rd, own,
):
    r = lax.axis_index("rt")
    c = lax.axis_index("ct")
    core = lax.rem(r, 2)
    x = r // 2
    sibling = r + 1 - 2 * core
    chip_peers = [2 * lax.rem(x + d, CHIPS) + core for d in range(1, CHIPS)]
    barrier = pltpu.get_barrier_semaphore()
    for d in range(1, NR):
        pl.semaphore_signal(barrier, inc=1, device_id=(lax.rem(r + d, NR), c), device_id_type=MESH)
    for e in range(1, NC):
        pl.semaphore_signal(barrier, inc=1, device_id=(r, lax.rem(c + e, NC)), device_id_type=MESH)

    pieces = three_parts(pan_ref[...])
    po[...] = jnp.dot(sel_ref[c], pieces, preferred_element_type=f32).reshape(NR, CAP, PANEL)
    ap[c] = pan_ref[...]
    pl.semaphore_wait(barrier, NR + NC - 2)

    def send(src, dst, ss, rs, rt, ct):
        copy = pltpu.make_async_remote_copy(
            src_ref=src, dst_ref=dst, send_sem=ss, recv_sem=rs, device_id=(rt, ct), device_id_type=MESH
        )
        copy.start()
        return copy

    def to_rt(src_of, dst, ss, rs):
        copies = []
        for d in range(1, NR):
            t = lax.rem(r + d, NR)
            copies.append(send(src_of(t), dst, ss.at[d - 1], rs.at[d - 1], t, c))
        return copies

    def wait_all(copies):
        for copy in copies:
            copy.wait()

    def start_columns(j):
        copies = []
        for e in range(1, NC):
            to = lax.rem(c + e, NC)
            copies.append(
                send(x_ref.at[j, to], fp.at[j, c], t1s.at[j, e - 1], t1r.at[j, e - 1], r, to)
            )
        fp[j, c] = x_ref[j, c]
        return copies

    local = []

    def route(j, copies):
        wait_all(copies)

        def one(s, carry):
            y = jnp.dot(sel_ref[s], three_parts(fp[j, s]), preferred_element_type=f32)
            routed[j, :, pl.ds(pl.multiple_of(s * CAP, CAP), CAP), :] = y.reshape(NR, CAP, QCOLS)
            return carry

        lax.fori_loop(0, NC, one, 0)
        here = fs_ref.at[r, :, pl.ds(j * QCOLS, QCOLS)]
        sends = to_rt(lambda t: routed.at[j, t], here, t2s.at[j], t2r.at[j])
        keep = pltpu.make_async_copy(routed.at[j, r], here, own.at[j])
        keep.start()
        local.append(keep)
        return sends

    panel = GatherCt(
        lambda h: pan_ref.at[pl.ds(h * SRC // 2, SRC // 2)],
        lambda h, o: ap.at[o, pl.ds(h * SRC // 2, SRC // 2)],
        r, c, a1s, a1r, a2s, a2r,
    )
    rows = GatherCt(
        lambda h: chunk.at[pl.ds(h * NR // 2, NR // 2)],
        lambda h, o: as_ref.at[pl.ds(h * NR // 2, NR // 2), o],
        r, c, c1s, c1r, c2s, c2r,
    )
    grams = GatherCt(
        lambda h: gsum.at[pl.ds(h * len(PAIRS) // 2, len(PAIRS) // 2)],
        lambda h, o: gbuf.at[o, pl.ds(h * len(PAIRS) // 2, len(PAIRS) // 2)],
        r, c, g1s, g1r, g2s, g2r,
    )

    panel.start()
    chunks = to_rt(lambda t: po.at[t], chunk.at[r], p1s, p1r)
    chunk[r] = po[r]
    columns = [start_columns(0)]
    panel.forward()
    columns.append(start_columns(1))
    panel.finish()
    columns.append(start_columns(2))
    columns.append(start_columns(3))

    whole = ap[...].reshape(NC * SRC, PANEL)
    apt[...] = whole.T
    for i in range(PANEL // LANES):
        block = jnp.dot(
            apt[i * LANES : (i + 1) * LANES, :],
            ap[:, :, i * LANES :].reshape(NC * SRC, PANEL - i * LANES),
            precision=highest,
            preferred_element_type=f32,
        )
        for j in range(i, PANEL // LANES):
            piece = block[:, (j - i) * LANES : (j - i + 1) * LANES]
            gpart[:, PAIRS.index((i, j))] = piece.reshape(NC, SUB, LANES)
    gram_sends = to_rt(lambda t: gpart.at[c], gin.at[r], p3s, p3r)
    gin[r] = gpart[c]

    routes = [route(0, columns[0])]
    wait_all(gram_sends)
    total = gin[0]
    for t in range(1, NR):
        total = total + gin[t]
    gsum[...] = total
    grams.start()
    gbuf[c] = total
    routes.append(route(1, columns[1]))
    grams.forward()
    wait_all(chunks)
    rows.start()
    keep = pltpu.make_async_copy(chunk, as_ref.at[:, c], own.at[QUARTERS])
    keep.start()
    local.append(keep)
    routes.append(route(2, columns[2]))
    grams.finish()
    for n, (i, j) in enumerate(PAIRS):
        work[i * LANES : (i + 1) * LANES, j * LANES : (j + 1) * LANES] = gbuf[:, n].reshape(LANES, LANES)
    ids = lax.broadcasted_iota(jnp.int32, (PANEL, PANEL), 0)
    lanes = lax.broadcasted_iota(jnp.int32, (PANEL, PANEL), 1)
    work[:, PANEL:] = jnp.where(ids == lanes, 1.0, 0.0).astype(f32)
    routes.append(route(3, columns[3]))
    rows.forward()

    def product(n, carry):
        i = n // QUARTERS
        j = lax.rem(n, QUARTERS)
        ah, al = two_parts(apt[pl.ds(pl.multiple_of(i * LANES, LANES), LANES), :])
        bh, bl = two_parts(fp[j].reshape(NC * SRC, QCOLS))
        y = jnp.dot(ah, bh, preferred_element_type=f32)
        y = y + jnp.dot(ah, bl, preferred_element_type=f32)
        y = y + jnp.dot(al, bh, preferred_element_type=f32)
        y = y.reshape(LANES // SLICE, SLICE, QCOLS)
        at = pl.ds(lax.rem(i, 2) * (LANES // SLICE), LANES // SLICE)
        part[i // 2, at, :, pl.ds(pl.multiple_of(j * QCOLS, QCOLS), QCOLS)] = y
        return carry

    lax.fori_loop(0, QUARTERS * (PANEL // LANES), product, 0)
    swap = send(part.at[1 - core], ain, sa, ra, sibling, c)

    factor_step(0, work, small)
    swap.wait()
    half[...] = part[core] + ain[...]
    spread = [
        send(half.at[peer // 2], bin_ref.at[d], sb.at[d], rb.at[d], peer, c)
        for d, peer in enumerate(chip_peers)
    ]
    factor_step(1, work, small)
    factor_step(2, work, small)
    wait_all(spread)
    mine[...] = (half[x] + bin_ref[0]) + (bin_ref[1] + bin_ref[2])
    spread = [
        send(mine, full.at[core, x], sc.at[d], rc.at[d], peer, c) for d, peer in enumerate(chip_peers)
    ]
    last = [send(mine, full.at[core, x], sd.at[CHIPS - 1], rd.at[CHIPS - 1], sibling, c)]
    full[core, x] = mine[...]
    factor_step(3, work, small)
    inv_ref[...] = work[:, PANEL:]
    for d, copy in enumerate(spread):
        copy.wait()
        owner = lax.rem(x + CHIPS - d - 1, CHIPS)
        last.append(
            send(full.at[core, owner], full.at[core, owner], sd.at[d], rd.at[d], sibling, c)
        )
    rows.finish()
    wait_all(last)
    sum_ref[...] = full[...].reshape(PANEL, BLOCK_COLS)
    for copies in routes:
        wait_all(copies)
    wait_all(local)


def factor_step(b, work, small):
    o = b * LANES
    lane = lax.broadcasted_iota(jnp.int32, (SUB, LANES), 1)
    sub = lax.broadcasted_iota(jnp.int32, (SUB, LANES), 0)
    block = [work[o + SUB * g : o + SUB * (g + 1), o : o + LANES] for g in range(LANES // SUB)]
    unit = [jnp.where(lane == sub + SUB * g, 1.0, 0.0).astype(f32) for g in range(LANES // SUB)]

    def write(g, v):
        small[SUB * g : SUB * (g + 1), :] = v

    inverse_of_block(block, unit, write)
    end = PANEL + o + LANES
    row = jnp.dot(
        small[...], work[o : o + LANES, o:end], precision=highest, preferred_element_type=f32
    )
    work[o : o + LANES, o:end] = row
    for p in range(o + LANES, PANEL, LANES):
        mult = row[:, p - o : p - o + LANES]
        work[p : p + LANES, p:end] = work[p : p + LANES, p:end] - jnp.dot(
            mult.T, row[:, p - o :], precision=highest, preferred_element_type=f32
        )


def build_front(columns, panel, select):
    slots = NC * CAP
    vmem = pltpu.VMEM
    dma = pltpu.SemaphoreType.DMA
    n = len(PAIRS)
    ring = [dma((2, SIDE - 1)), dma((2, SIDE - 1)), dma((2, SIDE, SIDE - 1)), dma((2, SIDE, SIDE - 1))]
    return pl.pallas_call(
        front_kernel,
        in_specs=[pl.BlockSpec(memory_space=pltpu.VMEM)] * 3,
        out_specs=[pl.BlockSpec(memory_space=pl.ANY)] * 2 + [pl.BlockSpec(memory_space=pltpu.VMEM)] * 2,
        out_shape=[
            jax.ShapeDtypeStruct((NR, slots, BLOCK_COLS), f32),
            jax.ShapeDtypeStruct((NR, NC, CAP, PANEL), f32),
            jax.ShapeDtypeStruct((PANEL, BLOCK_COLS), f32),
            jax.ShapeDtypeStruct((PANEL, PANEL), f32),
        ],
        scratch_shapes=[
            vmem((NR, CAP, PANEL), f32),
            vmem((NR, CAP, PANEL), f32),
            vmem((NC, SRC, PANEL), f32),
            vmem((PANEL, NC * SRC), f32),
            vmem((NC, n, SUB, LANES), f32),
            vmem((NR, n, SUB, LANES), f32),
            vmem((n, SUB, LANES), f32),
            vmem((NC, n, SUB, LANES), f32),
            vmem((QUARTERS, NC, SRC, QCOLS), f32),
            vmem((QUARTERS, NR, slots, QCOLS), f32),
            vmem((PANEL, 2 * PANEL), f32),
            vmem((LANES, LANES), f32),
            vmem((2, CHIPS, SLICE, BLOCK_COLS), f32),
            vmem((CHIPS, SLICE, BLOCK_COLS), f32),
            vmem((CHIPS, SLICE, BLOCK_COLS), f32),
            vmem((CHIPS - 1, SLICE, BLOCK_COLS), f32),
            vmem((SLICE, BLOCK_COLS), f32),
            vmem((2, CHIPS, SLICE, BLOCK_COLS), f32),
            dma((NR - 1,)),
            dma((NR - 1,)),
            *ring,
            *ring,
            *ring,
            dma((NR - 1,)),
            dma((NR - 1,)),
            dma((QUARTERS, NC - 1)),
            dma((QUARTERS, NC - 1)),
            dma((QUARTERS, NR - 1)),
            dma((QUARTERS, NR - 1)),
            dma(()),
            dma(()),
            dma((CHIPS - 1,)),
            dma((CHIPS - 1,)),
            dma((CHIPS - 1,)),
            dma((CHIPS - 1,)),
            dma((CHIPS,)),
            dma((CHIPS,)),
            dma((QUARTERS + 1,)),
        ],
        compiler_params=pltpu.CompilerParams(collective_id=0, has_side_effects=True),
        cost_estimate=pl.CostEstimate(
            flops=3_000_000_000, bytes_accessed=300_000_000, transcendentals=0
        ),
    )(columns, panel, select)


def tables(row_map, column_map, staircase, r, c):
    sources = NR * NC
    device_id = r * NC + c
    which_child = r // (NR // 2)
    tile = (row_map // ROWS_DEV).reshape(sources, SRC)
    same = tile[:, :, None] == tile[:, None, :]
    before = jnp.arange(SRC)[:, None] > jnp.arange(SRC)[None, :]
    rank = jnp.sum((same & before[None]).astype(jnp.int32), axis=2)
    slots = lax.dynamic_slice_in_dim(tile * CAP + rank, r * NC, NC)
    select = slots[:, None, :] == jnp.arange(NR * CAP, dtype=jnp.int32)[None, :, None]
    select = jnp.tile(select.astype(bf16), (1, 1, 3))
    local = row_map.reshape(sources, SRC) - r * ROWS_DEV
    hit = (tile == r)[:, :, None] & (rank[:, :, None] == jnp.arange(CAP)[None, None, :])
    front_of_slot = jnp.sum(jnp.where(hit, local[:, :, None] + 1, 0), axis=1).reshape(-1) - 1
    slot_of_front = jnp.sum(
        jnp.where(
            front_of_slot[None, :] == jnp.arange(ROWS_DEV, dtype=jnp.int32)[:, None],
            jnp.arange(sources * CAP, dtype=jnp.int32)[None, :],
            0,
        ),
        axis=1,
    )
    cmap = lax.dynamic_index_in_dim(column_map, which_child, 0, keepdims=False)
    stair = lax.dynamic_index_in_dim(staircase, which_child, 0, keepdims=False)
    blocks = jnp.arange(FRONT_BLOCKS, dtype=jnp.int32)
    high_part = ((cmap // LANES)[None, :] == blocks[:, None]).astype(bf16)
    low_part = ((cmap % LANES)[None, :] == jnp.arange(LANES, dtype=jnp.int32)[:, None]).astype(bf16)
    present = lax.dot_general(high_part, low_part, (((1,), (1,)), ((), ())), preferred_element_type=f32)
    upper = (jnp.arange(LANES)[:, None] < jnp.arange(LANES)[None, :]).astype(bf16)
    inside = jnp.dot(present.astype(bf16), upper, preferred_element_type=f32)
    counts = jnp.sum(present, axis=1)
    starts = jnp.sum(jnp.where(blocks[None, :] < blocks[:, None], counts[None, :], 0.0), axis=1)
    starts = starts.astype(jnp.int32)
    child_blocks = cmap.shape[0] // LANES
    q = jnp.minimum(starts // LANES, child_blocks - 2)
    code = starts[:, None] + inside.astype(jnp.int32) - q[:, None] * LANES
    code = jnp.where(present > 0.5, code, -1)
    first = lax.rem(device_id * SRC, row_map.shape[0] // 2)
    lim = jnp.repeat(stair, TILE // LANES, total_repeat_length=child_blocks) - first
    return select, slot_of_front, code, q, lim


def shards(children, row_map, column_map, staircase):
    r = lax.axis_index("rt")
    c = lax.axis_index("ct")
    select, slot_of_front, code, q, lim = tables(row_map, column_map, staircase, r, c)
    columns, panel = place(children, code, q, lim)
    arrived, panel_rows, projected, inverse = build_front(columns, panel, select)
    front_block = arrived.reshape(NR * NC * CAP, BLOCK_COLS)[slot_of_front]
    panel_block = panel_rows.reshape(NR * NC * CAP, PANEL)[slot_of_front]
    basis = lax.dot_general(
        inverse, panel_block, (((1,), (1,)), ((), ())), precision=high, preferred_element_type=f32
    )
    factor_rows = jnp.dot(inverse, projected, precision=high, preferred_element_type=f32)
    update = lax.dot_general(
        basis, factor_rows, (((0,), (0,)), ((), ())), precision=high, preferred_element_type=f32
    )
    return (factor_rows, basis, front_block - update)


def solution(mesh):
    placed = (P(("rt", "ct"), None), P(), P(), P())
    return jax.shard_map(
        shards,
        mesh=mesh,
        in_specs=placed,
        out_specs=(P(None, "ct"), P(None, "rt"), P("rt", "ct")),
        check_vma=False,
    )
```

time: 379 us -> 165 us (0.44); the launches traced: 372 us -> 163 us
  other arithmetic: 124 us -> 4.65 us
  Pallas kernels: 172 us -> 133 us
  matrix products: 32.5 us -> 13.7 us
  local copies, waits for them, and re-layouts: 29.1 us -> 11.2 us
  starting transfers between devices: 11.7 us -> 0 us
    another operation x17 -> x0, other arithmetic: 120 us -> none  [the longest x14 78.7 us: shards(): lower = jnp.linalg.cholesky(gram)]
    pallas_call x2 -> x1, Pallas kernels: 151 us -> 109 us  [build_front(): pl.pallas_call(front_kernel, in_specs=[pl.BlockSpec(memory_space=pltpu.VM...]
    another operation x19 -> x2, local copies, waits for them, and re-layouts: 15.2 us -> 0.93 us  [tables(): select = jnp.tile(select.astype(bf16), (1, 1, 3))]
    all_to_all x1 -> x0, starting transfers between devices: 11.7 us -> none  [shards(): lax.all_to_all(outgoing.reshape(NR * NC, CAP, BLOCK_COLS), ('rt', 'ct'),...]
    another operation x13 -> x0, matrix products: 11.2 us -> none  [the longest x7 5.68 us: shards(): jax.scipy.linalg.solve_triangular(lower, jnp.eye(PANEL, dtype=f32), lower...]
    dot_general x1 -> x0, matrix products: 7.04 us -> none  [shards(): lax.dot_general(panel_rows, arrived, (((0,), (0,)), ((), ())), precision=...]
  transfers between devices with their start and end apart: 1 -> 0, of which waited for: 0 -> 0; matrix products, arithmetic and copies ran while one was open for 42% -> 0% of each run, Pallas kernels for 30% -> 0%
where the time goes in v2:
time: 165 us; the launch traced here: 163 us
  Pallas kernels  133 us (81%)
  matrix products  13.7 us (8%)
  local copies, waits for them, and re-layouts  11.2 us (7%)
  other arithmetic  4.65 us (3%)
    pallas_call x1, Pallas kernels, build_front(): pl.pallas_call(front_kernel, in_specs=[pl.BlockSpec(memory_space=pltpu.VM...  109 us
    pallas_call x1, Pallas kernels, place(): pl.pallas_call(place_kernel, grid_spec=pltpu.PrefetchScalarGridSpec(num_s...  23.9 us
    gather x1, local copies, waits for them, and re-layouts, shards(): front_block = arrived.reshape(NR * NC * CAP, BLOCK_COLS)[slot_of_front]  5.35 us
    dot_general x1, matrix products, shards(): jnp.dot(inverse, projected, precision=high, preferred_element_type=f32)  5.21 us
    dot_general x1, matrix products, shards(): lax.dot_general(basis, factor_rows, (((0,), (0,)), ((), ())), precision=h...  3.36 us

profile of v2, /device:TPU:0, one launch (start us, length us, event | category | flops | bytes accessed | tf_op | source)
XLA Modules:
  0.0 163.3 jit_solution(9221275029176595536)
XLA Ops:
  0.7 0.6 copy-done
  1.3 0.7 pad_clamp_fusion.1
  2.0 1.2 gather_fusion
  3.2 0.5 broadcast_subtract_fusion.lim_ref
  3.7 0.7 subtract_add_fusion
  4.5 0.1 add.93
  4.5 0.1 copy.17
  4.6 0.1 reshape.135
  4.7 0.1 copy.11
  4.8 0.1 copy.16
  4.9 0.2 convert_reduce_fusion
  5.2 0.1 dynamic-slice_add_fusion
  5.2 0.1 copy.14
  5.3 0.1 copy.18
  5.4 0.1 sub.69
  5.5 0.3 select_reduce_fusion
  5.8 1.1 and_select_fusion.1
  7.0 0.1 and_select_fusion
  7.1 1.9 %fusion.14 = (f32[128]{0:T(128)S(1)}, f32[128,128]{0,1:T(8,128)S(1)}) fusion(s32[12288]{0:T(1024)S(1)} %bitcast.18, s32[12288]{0:T(1024)S(1)} %bitcast.19), kind=kOutput, calls=%fused_computation.55 | convolution fusion | flops 405815168 | bytes 164352 | tf_op jit(solution)/shard_map/dot_general | solution.py:525
  8.9 0.1 select_reduce_fusion.2
  9.0 0.6 broadcast_multiply_fusion
  9.7 0.1 copy.10
  9.7 0.8 fusion.5.code_ref
  10.6 0.1 fusion.6
  10.8 0.9 copy.15.sel_ref
  11.7 23.9 %shard_map.67 = (f32[4,16,32,256]{3,2,1,0:T(8,128)}, f32[32,512]{1,0:T(8,128)}) custom-call(s32[128]{0:T(128)} %get-tuple-element.28.q_ref, s32[96]{0:T(128)} %broadcast_subtract_fusion.lim_ref, f32[32,12288]{1,0:T(8,128)} %ch_ref.1, s32[128,128]{1,0:T(8,128)} %fusion.5.code_ref), custom_call_target="tpu_custom_call" | custom-call | flops 10000000 | bytes 4000000 | tf_op jit(solution)/shard_map/pallas_call | solution.py:69
  35.6 109.0 %shard_map.68 = (f32[8,128,1024]{2,1,0:T(8,128)}, f32[8,16,8,512]{3,2,1,0:T(8,128)}, f32[512,1024]{1,0:T(8,128)}, f32[512,512]{1,0:T(8,128)}) custom-call(f32[4,16,32,256]{3,2,1,0:T(8,128)} %get-tuple-element.21.x_ref, f32[32,512]{1,0:T(8,128)} %get-tuple-element.22.pan_ref, bf16[16,64,96]{2,1,0:T(8,128)(2,1)} %copy.15.sel_ref), custom_call_target="tpu_custom_call" | custom-call | flops 3000000000 | bytes 300000000 | tf_op jit(solution)/shard_map/pallas_call | solution.py:441
  144.6 5.2 %fusion.15 = f32[512,1024]{1,0:T(8,128)} fusion(f32[512,512]{1,0:T(8,128)} %get-tuple-element.23, f32[512,1024]{1,0:T(8,128)} %get-tuple-element.24), kind=kOutput, calls=%fused_computation.56 | convolution fusion | flops 1610612736 | bytes 5242880 | tf_op jit(solution)/shard_map/dot_general | solution.py:551
  149.8 2.3 %gather_fusion.1 = f32[512,512]{1,0:T(8,128)} fusion(f32[1024,512]{1,0:T(8,128)S(1)} %bitcast.16, s32[1024]{0:T(1024)S(1)} %pad_clamp_fusion), kind=kCustom, calls=%fused_computation.1 | custom fusion | bytes 2099200 | tf_op jit(solution)/shard_map/gather | solution.py:547
  152.1 5.4 %gather_fusion.2 = f32[512,1024]{1,0:T(8,128)S(1)} fusion(f32[1024,1024]{1,0:T(8,128)} %bitcast.15, s32[1024]{0:T(1024)S(1)} %pad_clamp_fusion), kind=kCustom, calls=%fused_computation.2 | custom fusion | bytes 4196352 | tf_op jit(solution)/shard_map/gather | solution.py:546
  157.5 2.4 %fusion.16 = f32[512,512]{1,0:T(8,128)S(1)} fusion(f32[512,512]{1,0:T(8,128)S(1)} %copy-done.3, f32[512,512]{1,0:T(8,128)} %gather_fusion.1), kind=kOutput, calls=%fused_computation.57 | convolution fusion | flops 805306368 | bytes 3145728 | tf_op jit(solution)/shard_map/dot_general | solution.py:548
  160.0 3.4 %convolution_subtract_fusion = f32[512,1024]{1,0:T(8,128)} fusion(f32[512,1024]{1,0:T(8,128)S(1)} %gather_fusion.2, f32[512,512]{1,0:T(8,128)S(1)} %fusion.16, f32[512,1024]{1,0:T(8,128)S(1)} %copy-done.2), kind=kOutput, calls=%fused_computation.10 | convolution fusion | flops 1611137024 | bytes 7340032 | tf_op jit(solution)/shard_map/dot_general | solution.py:552
  (18 shorter events, 0.2 us)
Async XLA Ops:
  0.6 0.7 copy-start
  144.6 5.2 %copy-start.1 = (f32[8,16,8,512]{3,2,1,0:T(8,128)S(1)}, f32[8,16,8,512]{3,2,1,0:T(8,128)}, u32[]{:S(2)}) copy-start(f32[8,16,8,512]{3,2,1,0:T(8,128)} %get-tuple-element.25) | copy-start | bytes 6291460
  152.1 5.4 %copy-start.3 = (f32[512,512]{1,0:T(8,128)S(1)}, f32[512,512]{1,0:T(8,128)}, u32[]{:S(2)}) copy-start(f32[512,512]{1,0:T(8,128)} %get-tuple-element.23) | copy-start | bytes 3145732
  157.5 2.4 %copy-start.2 = (f32[512,1024]{1,0:T(8,128)S(1)}, f32[512,1024]{1,0:T(8,128)}, u32[]{:S(2)}) copy-start(f32[512,1024]{1,0:T(8,128)} %fusion.15) | copy-start | bytes 6291460
  159.9 3.4 %copy-start.4 = (f32[512,512]{1,0:T(8,128)}, f32[512,512]{1,0:T(8,128)S(1)}, u32[]{:S(2)}) copy-start(f32[512,512]{1,0:T(8,128)S(1)} %fusion.16) | copy-start | bytes 3145732

commit v3 on v2

--- a/solution.py
+++ b/solution.py
@@ -33,59 +33,134 @@
 MESH = pl.DeviceIdType.MESH
 
 
-def place_kernel(q_ref, lim_ref, ch_ref, code_ref, out_ref, panel_ref):
-    step = pl.program_id(0)
-    row_ids = lax.broadcasted_iota(jnp.int32, (SUB, LANES), 0)
-    per_step = BLOCK_COLS // LANES
-    for sub in range(per_step):
-        b = step * per_step + sub
-        q = q_ref[b]
-        start = pl.multiple_of(q * LANES, LANES)
-        after = pl.multiple_of(start + LANES, LANES)
-        code = jnp.broadcast_to(code_ref[pl.ds(b, 1), :], (SUB, LANES))
-        lane = jnp.bitwise_and(code, LANES - 1)
-        first = lim_ref[q]
-        second = lim_ref[q + 1]
-        limit = jnp.where(code < LANES, first, second)
-        limit = jnp.where(code < 0, 0, limit)
-        quarter, offset = divmod(sub * LANES, QCOLS)
-        for g in range(SRC // SUB):
-            v0 = ch_ref[g * SUB : (g + 1) * SUB, pl.ds(start, LANES)]
-            v1 = ch_ref[g * SUB : (g + 1) * SUB, pl.ds(after, LANES)]
-            g0 = jnp.take_along_axis(v0, lane, axis=1)
-            g1 = jnp.take_along_axis(v1, lane, axis=1)
-            x = jnp.where(code < LANES, g0, g1)
-            x = jnp.where(row_ids + g * SUB < limit, x, 0.0)
-            out_ref[quarter, 0, g * SUB : (g + 1) * SUB, offset : offset + LANES] = x
-            if sub < PANEL // LANES:
-
-                @pl.when(step == 0)
-                def _():
-                    panel_ref[g * SUB : (g + 1) * SUB, sub * LANES : (sub + 1) * LANES] = x
-
-
-def place(children, code, q, lim):
-    child_cols = children.shape[1]
+def table_kernel(
+    stair_ref, row_ref, col_ref, ch_ref, x_ref, pan_ref, slot_ref, front_ref, code_ref, qv_ref, q_ref, sem
+):
+    r = lax.axis_index("rt")
+    c = lax.axis_index("ct")
+    child = r // (NR // 2)
+    child_cols = col_ref.shape[1]
+    rows = row_ref.shape[0]
+    sub = lax.broadcasted_iota(jnp.int32, (LANES, LANES), 0)
+    lane = lax.broadcasted_iota(jnp.int32, (LANES, LANES), 1)
+
+    step = child_cols // 6
+    ids = lax.broadcasted_iota(jnp.int32, (LANES, step), 0)
+    present = jnp.zeros((LANES, LANES), f32)
+    for n in range(6):
+        cm = col_ref[pl.ds(child, 1), n * step : (n + 1) * step]
+        cm = jnp.broadcast_to(cm, (LANES, step))
+        upper = (jnp.right_shift(cm, 7) == ids).astype(f32).astype(bf16)
+        lower = (jnp.bitwise_and(cm, LANES - 1) == ids).astype(f32).astype(bf16)
+        present = present + lax.dot_general(
+            upper, lower, (((1,), (1,)), ((), ())), preferred_element_type=f32
+        )
+    flags = present.astype(bf16)
+    before = (sub < lane).astype(f32).astype(bf16)
+    inside = jnp.dot(flags, before, preferred_element_type=f32)
+    above = jnp.dot((lane < sub).astype(f32).astype(bf16), flags, preferred_element_type=f32)
+    starts = jnp.sum(above, axis=1, keepdims=True).astype(jnp.int32)
+    last = child_cols // LANES - 2
+    q = jnp.minimum(jnp.right_shift(starts, 7), last)
+    code = starts - q * LANES + inside.astype(jnp.int32)
+    code_ref[...] = jnp.where(present > 0.5, code, -1)
+    across = lax.dot_general(
+        jnp.ones((SUB, LANES), bf16), above.astype(bf16), (((1,), (1,)), ((), ())),
+        preferred_element_type=f32,
+    )
+    qv_ref[...] = jnp.minimum(jnp.right_shift(across.astype(jnp.int32), 7), last)
+
+    rm = row_ref[...]
+    tile = jnp.right_shift(rm, 9)
+    group = jnp.right_shift(sub, 5) == jnp.right_shift(lane, 5)
+    earlier = (group & (sub < lane)).astype(f32).astype(bf16)
+    slot = jnp.zeros((rows, LANES), jnp.int32)
+    for t in range(NR):
+        hit = tile == t
+        rank = jnp.dot(hit.astype(f32).astype(bf16), earlier, preferred_element_type=f32)
+        slot = jnp.where(hit, t * CAP + rank.astype(jnp.int32), slot)
+    slot_ref[...] = slot
+    local = (rm - r * ROWS_DEV + 1).astype(f32)
+    small_sub = lax.broadcasted_iota(jnp.int32, (LANES, SRC), 0)
+    small_lane = lax.broadcasted_iota(jnp.int32, (LANES, SRC), 1)
+    packed = jnp.zeros((rows, SRC), f32)
+    for k in range(CAP):
+        value = jnp.where(slot == r * CAP + k, local, 0.0)
+        to = (jnp.right_shift(small_sub, 5) * CAP + k == small_lane).astype(f32)
+        packed = packed + jnp.dot(value, to, precision=highest, preferred_element_type=f32)
+    slots = NR * NC * CAP
+    wide_sub = lax.broadcasted_iota(jnp.int32, (SRC, slots), 0)
+    wide_lane = lax.broadcasted_iota(jnp.int32, (SRC, slots), 1)
+    repeat = (jnp.bitwise_and(wide_lane, SRC - 1) == wide_sub).astype(f32)
+    spread = jnp.dot(packed, repeat, precision=highest, preferred_element_type=f32)
+    flat = jnp.where(jnp.right_shift(wide_lane, 5) == wide_sub, spread, 0.0)
+    flat = jnp.sum(flat, axis=0, keepdims=True)
+    front_ref[...] = jnp.broadcast_to(flat.astype(jnp.int32) - 1, (SUB, slots))
+    fetch = pltpu.make_async_copy(qv_ref, q_ref, sem)
+    fetch.start()
+
+    first_row = lax.rem((r * NC + c) * SRC, NR * NC * SRC // 2)
+    for t in range(PANEL // TILE):
+        at = slice(t * TILE, (t + 1) * TILE)
+        ids = lax.broadcasted_iota(jnp.int32, (SRC, TILE), 0)
+        pan_ref[:, at] = jnp.where(ids + first_row < stair_ref[child, t], ch_ref[:, at], 0.0)
+    fetch.wait()
+    sub_ids = lax.broadcasted_iota(jnp.int32, (SUB, LANES), 0) + first_row
+    halves = QCOLS // LANES
+
+    def one(m, carry):
+        j = m // (NC // 2)
+        n = lax.rem(m, NC // 2)
+        found = []
+        for cc in range(2):
+            for h in range(halves):
+                b = (n * 2 + cc) * (BLOCK_COLS // LANES) + j * halves + h
+                q = q_ref[0, b]
+                start = pl.multiple_of(q * LANES, LANES)
+                after = pl.multiple_of(start + LANES, LANES)
+                code = jnp.broadcast_to(code_ref[pl.ds(b, 1), :], (SUB, LANES))
+                lane = jnp.bitwise_and(code, LANES - 1)
+                limit = jnp.where(
+                    code < LANES,
+                    stair_ref[child, q // (TILE // LANES)],
+                    stair_ref[child, (q + 1) // (TILE // LANES)],
+                )
+                limit = jnp.where(code < 0, 0, limit)
+                for g in range(SRC // SUB):
+                    v0 = ch_ref[g * SUB : (g + 1) * SUB, pl.ds(start, LANES)]
+                    v1 = ch_ref[g * SUB : (g + 1) * SUB, pl.ds(after, LANES)]
+                    g0 = jnp.take_along_axis(v0, lane, axis=1)
+                    g1 = jnp.take_along_axis(v1, lane, axis=1)
+                    v = jnp.where(code < LANES, g0, g1)
+                    found.append((cc, h, g, jnp.where(sub_ids + g * SUB < limit, v, 0.0)))
+        for cc, h, g, v in found:
+            x_ref[j, n * 2 + cc, g * SUB : (g + 1) * SUB, h * LANES : (h + 1) * LANES] = v
+        return carry
+
+    lax.fori_loop(0, QUARTERS * NC // 2, one, 0)
+
+
+def place_columns(children, row_map, column_map, staircase):
+    vmem = pl.BlockSpec(memory_space=pltpu.VMEM)
+    rows = row_map.shape[0] // LANES
     return pl.pallas_call(
-        place_kernel,
-        grid_spec=pltpu.PrefetchScalarGridSpec(
-            num_scalar_prefetch=2,
-            grid=(NC,),
-            in_specs=[
-                pl.BlockSpec((SRC, child_cols), lambda i, *_: (0, 0)),
-                pl.BlockSpec((FRONT_BLOCKS, LANES), lambda i, *_: (0, 0)),
-            ],
-            out_specs=[
-                pl.BlockSpec((QUARTERS, 1, SRC, QCOLS), lambda i, *_: (0, i, 0, 0)),
-                pl.BlockSpec((SRC, PANEL), lambda i, *_: (0, 0)),
-            ],
-        ),
+        table_kernel,
+        in_specs=[pl.BlockSpec(memory_space=pltpu.SMEM)] + [vmem] * 3,
+        out_specs=[vmem] * 4,
         out_shape=[
             jax.ShapeDtypeStruct((QUARTERS, NC, SRC, QCOLS), f32),
             jax.ShapeDtypeStruct((SRC, PANEL), f32),
+            jax.ShapeDtypeStruct((rows, LANES), jnp.int32),
+            jax.ShapeDtypeStruct((SUB, NR * NC * CAP), jnp.int32),
         ],
-        cost_estimate=pl.CostEstimate(flops=10_000_000, bytes_accessed=4_000_000, transcendentals=0),
-    )(q, lim, children, code)
+        scratch_shapes=[
+            pltpu.VMEM((FRONT_BLOCKS, LANES), jnp.int32),
+            pltpu.VMEM((SUB, FRONT_BLOCKS), jnp.int32),
+            pltpu.SMEM((SUB, FRONT_BLOCKS), jnp.int32),
+            pltpu.SemaphoreType.DMA,
+        ],
+        cost_estimate=pl.CostEstimate(flops=400_000_000, bytes_accessed=4_000_000, transcendentals=0),
+    )(staircase, row_map.reshape(rows, LANES), column_map, children)
 
 
 def across_lanes(v, lane):
@@ -226,11 +301,12 @@
 
 
 def front_kernel(
-    x_ref, pan_ref, sel_ref, fs_ref, as_ref, sum_ref, inv_ref,
-    po, chunk, ap, apt, gpart, gin, gsum, gbuf, fp, routed, work, small,
+    x_ref, pan_ref, slot_ref, order_ref,
+    front_ref, rows_ref, sum_ref, inv_ref,
+    sel_ref, fs_ref, as_ref, perm, parts, po, chunk, ap, apt, gpart, gin, gsum, gbuf, fp, routed, work, small,
     part, ain, half, bin_ref, mine, full,
     p1s, p1r, a1s, a1r, a2s, a2r, c1s, c1r, c2s, c2r, g1s, g1r, g2s, g2r, p3s, p3r,
-    t1s, t1r, t2s, t2r, sa, ra, sb, rb, sc, rc, sd, rd, own,
+    t1s, t1r, t2s, t2r, sa, ra, sb, rb, sc, rc, sd, rd,
 ):
     r = lax.axis_index("rt")
     c = lax.axis_index("ct")
@@ -244,9 +320,6 @@
     for e in range(1, NC):
         pl.semaphore_signal(barrier, inc=1, device_id=(r, lax.rem(c + e, NC)), device_id_type=MESH)
 
-    pieces = three_parts(pan_ref[...])
-    po[...] = jnp.dot(sel_ref[c], pieces, preferred_element_type=f32).reshape(NR, CAP, PANEL)
-    ap[c] = pan_ref[...]
     pl.semaphore_wait(barrier, NR + NC - 2)
 
     def send(src, dst, ss, rs, rt, ct):
@@ -266,6 +339,20 @@
     def wait_all(copies):
         for copy in copies:
             copy.wait()
+
+    def selections():
+        lane = lax.broadcasted_iota(jnp.int32, (NR * CAP, LANES), 1)
+        ids = lax.broadcasted_iota(jnp.int32, (NR * CAP, LANES), 0)
+        per = LANES // SRC
+        for u in range(NC // per):
+            row = jnp.broadcast_to(slot_ref[pl.ds(r * (NC // per) + u, 1), :], (NR * CAP, LANES))
+            for v in range(per):
+                turned = [
+                    pltpu.roll(row, (g - v) % per * SRC, 1) if g != v else row for g in range(3)
+                ]
+                slots = jnp.where(lane < SRC, turned[0], jnp.where(lane < 2 * SRC, turned[1], turned[2]))
+                chosen = (slots == ids).astype(f32).astype(bf16)
+                sel_ref[u * per + v] = chosen[:, : 3 * SRC]
 
     def start_columns(j):
         copies = []
@@ -277,23 +364,64 @@
         fp[j, c] = x_ref[j, c]
         return copies
 
-    local = []
-
     def route(j, copies):
         wait_all(copies)
 
-        def one(s, carry):
-            y = jnp.dot(sel_ref[s], three_parts(fp[j, s]), preferred_element_type=f32)
-            routed[j, :, pl.ds(pl.multiple_of(s * CAP, CAP), CAP), :] = y.reshape(NR, CAP, QCOLS)
+        def four(n, carry):
+            done = []
+            for i in range(4):
+                s = n * 4 + i
+                y = jnp.dot(sel_ref[s], three_parts(fp[j, s]), preferred_element_type=f32)
+                done.append((s, y))
+            for s, y in done:
+                at = pl.ds(pl.multiple_of(s * CAP, CAP), CAP)
+                routed[j, :, at, :] = y.reshape(NR, CAP, QCOLS)
             return carry
 
-        lax.fori_loop(0, NC, one, 0)
-        here = fs_ref.at[r, :, pl.ds(j * QCOLS, QCOLS)]
-        sends = to_rt(lambda t: routed.at[j, t], here, t2s.at[j], t2r.at[j])
-        keep = pltpu.make_async_copy(routed.at[j, r], here, own.at[j])
-        keep.start()
-        local.append(keep)
+        lax.fori_loop(0, NC // 4, four, 0)
+        sends = to_rt(lambda t: routed.at[j, t], fs_ref.at[j, r], t2s.at[j], t2r.at[j])
+        fs_ref[j, r] = routed[j, r]
         return sends
+
+    def order(load, store, width):
+        def split(n, carry):
+            at = pl.ds(pl.multiple_of(n * LANES, LANES), LANES)
+            rest = load(n)
+            for p in range(3):
+                piece = rest.astype(bf16)
+                parts[p, at, :width] = piece
+                rest = rest - piece.astype(f32)
+            return carry
+
+        lax.fori_loop(0, NR, split, 0)
+
+        def rows_of(n, carry):
+            at = pl.ds(pl.multiple_of(n * LANES, LANES), LANES)
+            y = jnp.dot(perm[at, :], parts[0, :, :width], preferred_element_type=f32)
+            y = y + jnp.dot(perm[at, :], parts[1, :, :width], preferred_element_type=f32)
+            y = y + jnp.dot(perm[at, :], parts[2, :, :width], preferred_element_type=f32)
+            store(at, y)
+            return carry
+
+        lax.fori_loop(0, ROWS_DEV // LANES, rows_of, 0)
+
+    def order_columns(j, copies):
+        wait_all(copies)
+
+        def store(at, y):
+            front_ref[at, j * QCOLS : (j + 1) * QCOLS] = y
+
+        order(lambda n: fs_ref[j, n], store, QCOLS)
+
+    def make_perm():
+        def one(n, carry):
+            at = pl.ds(pl.multiple_of(n * LANES, LANES), LANES)
+            shape = (LANES, NR * NC * CAP)
+            ids = lax.broadcasted_iota(jnp.int32, shape, 0) + n * LANES
+            perm[at, :] = (jnp.broadcast_to(order_ref[0:1, :], shape) == ids).astype(f32).astype(bf16)
+            return carry
+
+        lax.fori_loop(0, ROWS_DEV // LANES, one, 0)
 
     panel = GatherCt(
         lambda h: pan_ref.at[pl.ds(h * SRC // 2, SRC // 2)],
@@ -312,15 +440,17 @@
     )
 
     panel.start()
-    chunks = to_rt(lambda t: po.at[t], chunk.at[r], p1s, p1r)
-    chunk[r] = po[r]
+    ap[c] = pan_ref[...]
     columns = [start_columns(0)]
     panel.forward()
+    selections()
     columns.append(start_columns(1))
     panel.finish()
     columns.append(start_columns(2))
     columns.append(start_columns(3))
-
+    po[...] = jnp.dot(
+        sel_ref[c], three_parts(pan_ref[...]), preferred_element_type=f32
+    ).reshape(NR, CAP, PANEL)
     whole = ap[...].reshape(NC * SRC, PANEL)
     apt[...] = whole.T
     for i in range(PANEL // LANES):
@@ -335,6 +465,8 @@
             gpart[:, PAIRS.index((i, j))] = piece.reshape(NC, SUB, LANES)
     gram_sends = to_rt(lambda t: gpart.at[c], gin.at[r], p3s, p3r)
     gin[r] = gpart[c]
+    chunks = to_rt(lambda t: po.at[t], chunk.at[r], p1s, p1r)
+    chunk[r] = po[r]
 
     routes = [route(0, columns[0])]
     wait_all(gram_sends)
@@ -348,9 +480,7 @@
     grams.forward()
     wait_all(chunks)
     rows.start()
-    keep = pltpu.make_async_copy(chunk, as_ref.at[:, c], own.at[QUARTERS])
-    keep.start()
-    local.append(keep)
+    as_ref[:, c] = chunk[...]
     routes.append(route(2, columns[2]))
     grams.finish()
     for n, (i, j) in enumerate(PAIRS):
@@ -384,8 +514,9 @@
         send(half.at[peer // 2], bin_ref.at[d], sb.at[d], rb.at[d], peer, c)
         for d, peer in enumerate(chip_peers)
     ]
+    make_perm()
     factor_step(1, work, small)
-    factor_step(2, work, small)
+    order_columns(0, routes[0])
     wait_all(spread)
     mine[...] = (half[x] + bin_ref[0]) + (bin_ref[1] + bin_ref[2])
     spread = [
@@ -393,6 +524,7 @@
     ]
     last = [send(mine, full.at[core, x], sd.at[CHIPS - 1], rd.at[CHIPS - 1], sibling, c)]
     full[core, x] = mine[...]
+    factor_step(2, work, small)
     factor_step(3, work, small)
     inv_ref[...] = work[:, PANEL:]
     for d, copy in enumerate(spread):
@@ -402,11 +534,20 @@
             send(full.at[core, owner], full.at[core, owner], sd.at[d], rd.at[d], sibling, c)
         )
     rows.finish()
+
+    def store_rows(lane_at):
+        def store(at, y):
+            rows_ref[at, lane_at : lane_at + QCOLS] = y
+
+        return store
+
+    for n in range(PANEL // QCOLS):
+        at = slice(n * QCOLS, (n + 1) * QCOLS)
+        order(lambda t: as_ref[t].reshape(NC * CAP, PANEL)[:, at], store_rows(n * QCOLS), QCOLS)
+    for j in range(1, QUARTERS):
+        order_columns(j, routes[j])
     wait_all(last)
     sum_ref[...] = full[...].reshape(PANEL, BLOCK_COLS)
-    for copies in routes:
-        wait_all(copies)
-    wait_all(local)
 
 
 def factor_step(b, work, small):
@@ -432,7 +573,7 @@
         )
 
 
-def build_front(columns, panel, select):
+def build_front(columns, panel, slot, order):
     slots = NC * CAP
     vmem = pltpu.VMEM
     dma = pltpu.SemaphoreType.DMA
@@ -440,15 +581,20 @@
     ring = [dma((2, SIDE - 1)), dma((2, SIDE - 1)), dma((2, SIDE, SIDE - 1)), dma((2, SIDE, SIDE - 1))]
     return pl.pallas_call(
         front_kernel,
-        in_specs=[pl.BlockSpec(memory_space=pltpu.VMEM)] * 3,
-        out_specs=[pl.BlockSpec(memory_space=pl.ANY)] * 2 + [pl.BlockSpec(memory_space=pltpu.VMEM)] * 2,
+        in_specs=[pl.BlockSpec(memory_space=pltpu.VMEM)] * 4,
+        out_specs=[pl.BlockSpec(memory_space=pltpu.VMEM)] * 4,
         out_shape=[
-            jax.ShapeDtypeStruct((NR, slots, BLOCK_COLS), f32),
-            jax.ShapeDtypeStruct((NR, NC, CAP, PANEL), f32),
+            jax.ShapeDtypeStruct((ROWS_DEV, BLOCK_COLS), f32),
+            jax.ShapeDtypeStruct((ROWS_DEV, PANEL), f32),
             jax.ShapeDtypeStruct((PANEL, BLOCK_COLS), f32),
             jax.ShapeDtypeStruct((PANEL, PANEL), f32),
         ],
         scratch_shapes=[
+            vmem((NC, NR * CAP, 3 * SRC), bf16),
+            vmem((QUARTERS, NR, slots, QCOLS), f32),
+            vmem((NR, NC, CAP, PANEL), f32),
+            vmem((ROWS_DEV, NR * slots), bf16),
+            vmem((3, NR * slots, QCOLS), bf16),
             vmem((NR, CAP, PANEL), f32),
             vmem((NR, CAP, PANEL), f32),
             vmem((NC, SRC, PANEL), f32),
@@ -486,65 +632,17 @@
             dma((CHIPS - 1,)),
             dma((CHIPS,)),
             dma((CHIPS,)),
-            dma((QUARTERS + 1,)),
         ],
         compiler_params=pltpu.CompilerParams(collective_id=0, has_side_effects=True),
         cost_estimate=pl.CostEstimate(
             flops=3_000_000_000, bytes_accessed=300_000_000, transcendentals=0
         ),
-    )(columns, panel, select)
-
-
-def tables(row_map, column_map, staircase, r, c):
-    sources = NR * NC
-    device_id = r * NC + c
-    which_child = r // (NR // 2)
-    tile = (row_map // ROWS_DEV).reshape(sources, SRC)
-    same = tile[:, :, None] == tile[:, None, :]
-    before = jnp.arange(SRC)[:, None] > jnp.arange(SRC)[None, :]
-    rank = jnp.sum((same & before[None]).astype(jnp.int32), axis=2)
-    slots = lax.dynamic_slice_in_dim(tile * CAP + rank, r * NC, NC)
-    select = slots[:, None, :] == jnp.arange(NR * CAP, dtype=jnp.int32)[None, :, None]
-    select = jnp.tile(select.astype(bf16), (1, 1, 3))
-    local = row_map.reshape(sources, SRC) - r * ROWS_DEV
-    hit = (tile == r)[:, :, None] & (rank[:, :, None] == jnp.arange(CAP)[None, None, :])
-    front_of_slot = jnp.sum(jnp.where(hit, local[:, :, None] + 1, 0), axis=1).reshape(-1) - 1
-    slot_of_front = jnp.sum(
-        jnp.where(
-            front_of_slot[None, :] == jnp.arange(ROWS_DEV, dtype=jnp.int32)[:, None],
-            jnp.arange(sources * CAP, dtype=jnp.int32)[None, :],
-            0,
-        ),
-        axis=1,
-    )
-    cmap = lax.dynamic_index_in_dim(column_map, which_child, 0, keepdims=False)
-    stair = lax.dynamic_index_in_dim(staircase, which_child, 0, keepdims=False)
-    blocks = jnp.arange(FRONT_BLOCKS, dtype=jnp.int32)
-    high_part = ((cmap // LANES)[None, :] == blocks[:, None]).astype(bf16)
-    low_part = ((cmap % LANES)[None, :] == jnp.arange(LANES, dtype=jnp.int32)[:, None]).astype(bf16)
-    present = lax.dot_general(high_part, low_part, (((1,), (1,)), ((), ())), preferred_element_type=f32)
-    upper = (jnp.arange(LANES)[:, None] < jnp.arange(LANES)[None, :]).astype(bf16)
-    inside = jnp.dot(present.astype(bf16), upper, preferred_element_type=f32)
-    counts = jnp.sum(present, axis=1)
-    starts = jnp.sum(jnp.where(blocks[None, :] < blocks[:, None], counts[None, :], 0.0), axis=1)
-    starts = starts.astype(jnp.int32)
-    child_blocks = cmap.shape[0] // LANES
-    q = jnp.minimum(starts // LANES, child_blocks - 2)
-    code = starts[:, None] + inside.astype(jnp.int32) - q[:, None] * LANES
-    code = jnp.where(present > 0.5, code, -1)
-    first = lax.rem(device_id * SRC, row_map.shape[0] // 2)
-    lim = jnp.repeat(stair, TILE // LANES, total_repeat_length=child_blocks) - first
-    return select, slot_of_front, code, q, lim
+    )(columns, panel, slot, order)
 
 
 def shards(children, row_map, column_map, staircase):
-    r = lax.axis_index("rt")
-    c = lax.axis_index("ct")
-    select, slot_of_front, code, q, lim = tables(row_map, column_map, staircase, r, c)
-    columns, panel = place(children, code, q, lim)
-    arrived, panel_rows, projected, inverse = build_front(columns, panel, select)
-    front_block = arrived.reshape(NR * NC * CAP, BLOCK_COLS)[slot_of_front]
-    panel_block = panel_rows.reshape(NR * NC * CAP, PANEL)[slot_of_front]
+    placed = place_columns(children, row_map, column_map, staircase)
+    front_block, panel_block, projected, inverse = build_front(*placed)
     basis = lax.dot_general(
         inverse, panel_block, (((1,), (1,)), ((), ())), precision=high, preferred_element_type=f32
     )

time: 165 us -> 137 us (0.83)
  local copies, waits for them, and re-layouts: 11.2 us -> 1.29 us
  Pallas kernels: 133 us -> 126 us
  matrix products: 13.7 us -> 8.31 us
  other arithmetic: 4.65 us -> 0 us
    pallas_call x1, Pallas kernels: 23.9 us -> 9.89 us  [place_columns(): pl.pallas_call(table_kernel, in_specs=[pl.BlockSpec(memory_space=pltpu.SM...]
    gather x3 -> x0, local copies, waits for them, and re-layouts: 8.9 us -> none  [the longest x1 5.35 us: shards(): front_block = arrived.reshape(NR * NC * CAP, BLOCK_COLS)[slot_of_front]]
    pallas_call x1, Pallas kernels: 109 us -> 117 us  [build_front(): pl.pallas_call(front_kernel, in_specs=[pl.BlockSpec(memory_space=pltpu.VM...]
    dot_general x2 -> x0, matrix products: 2.68 us -> none  [the longest x1 1.85 us: tables(): lax.dot_general(high_part, low_part, (((1,), (1,)), ((), ())), preferred_...]
where the time goes in v3:
time: 137 us
  Pallas kernels  126 us (92%)
  matrix products  8.31 us (6%)
    pallas_call x1, Pallas kernels, build_front(): pl.pallas_call(front_kernel, in_specs=[pl.BlockSpec(memory_space=pltpu.VM...  117 us
    pallas_call x1, Pallas kernels, place_columns(): pl.pallas_call(table_kernel, in_specs=[pl.BlockSpec(memory_space=pltpu.SM...  9.89 us
    dot_general x1, matrix products, shards(): jnp.dot(inverse, projected, precision=high, preferred_element_type=f32)  3.91 us
    dot_general x1, matrix products, shards(): lax.dot_general(basis, factor_rows, (((0,), (0,)), ((), ())), precision=h...  3.33 us

profile of v3, /device:TPU:0, one launch (start us, length us, event | category | flops | bytes accessed | tf_op | source)
XLA Modules:
  0.0 136.7 jit_solution(363486897884025013)
XLA Ops:
  0.6 9.9 %shard_map.67 = (f32[4,16,32,256]{3,2,1,0:T(8,128)}, f32[32,512]{1,0:T(8,128)}, s32[32,128]{1,0:T(8,128)}, s32[8,1024]{1,0:T(8,128)}) custom-call(s32[2,48]{1,0:T(2,128)} %stair_ref.1, s32[32,128]{1,0:T(8,128)} %bitcast.7, s32[2,12288]{1,0:T(2,128)} %col_ref.1, f32[32,12288]{1,0:T(8,128)} %ch_ref.1), custom_call_target="tpu_custom_call" | custom-call | flops 400000000 | bytes 4000000 | tf_op jit(solution)/shard_map/pallas_call | solution.py:146
  10.5 116.5 %shard_map.68 = (f32[512,1024]{1,0:T(8,128)}, f32[512,512]{1,0:T(8,128)}, f32[512,1024]{1,0:T(8,128)}, f32[512,512]{1,0:T(8,128)}) custom-call(f32[4,16,32,256]{3,2,1,0:T(8,128)} %get-tuple-element.11.x_ref, f32[32,512]{1,0:T(8,128)} %get-tuple-element.12.pan_ref, s32[32,128]{1,0:T(8,128)} %get-tuple-element.13.slot_ref, s32[8,1024]{1,0:T(8,128)} %get-tuple-element.14.order_ref), custom_call_target="tpu_custom_call" | custom-call | flops 3000000000 | bytes 300000000 | tf_op jit(solution)/shard_map/pallas_call | solution.py:582
  127.0 0.0 copy-start.1
  127.0 0.0 copy-start.4
  127.1 3.9 %fusion = f32[512,1024]{1,0:T(8,128)S(1)} fusion(f32[512,512]{1,0:T(8,128)} %get-tuple-element.15, f32[512,1024]{1,0:T(8,128)} %get-tuple-element.16), kind=kOutput, calls=%fused_computation.1 | convolution fusion | flops 1610612736 | bytes 5242880 | tf_op jit(solution)/shard_map/dot_general | solution.py:649
  131.0 0.0 copy-done.1
  131.0 0.0 copy-done.4
  131.0 0.0 copy-start
  131.0 0.0 copy-start.3
  131.0 1.1 fusion.1
  132.1 1.3 copy-done.3
  133.4 0.0 copy-start.2
  133.4 3.3 %convolution_subtract_fusion = f32[512,1024]{1,0:T(8,128)} fusion(f32[512,1024]{1,0:T(8,128)S(1)} %copy-done.3, f32[512,512]{1,0:T(8,128)S(1)} %fusion.1, f32[512,1024]{1,0:T(8,128)S(1)} %fusion), kind=kOutput, calls=%fused_computation | convolution fusion | flops 1611137024 | bytes 7340032 | tf_op jit(solution)/shard_map/dot_general | solution.py:650
  136.7 0.0 copy-done
  136.7 0.0 copy-done.2
Async XLA Ops:
  127.0 3.9 %copy-start.1 = (f32[512,512]{1,0:T(8,128)S(1)}, f32[512,512]{1,0:T(8,128)}, u32[]{:S(2)}) copy-start(f32[512,512]{1,0:T(8,128)} %get-tuple-element.15) | copy-start | bytes 3145732
  127.0 3.9 %copy-start.4 = (f32[512,512]{1,0:T(8,128)S(1)}, f32[512,512]{1,0:T(8,128)}, u32[]{:S(2)}) copy-start(f32[512,512]{1,0:T(8,128)} %get-tuple-element.17) | copy-start | bytes 3145732
  131.0 5.7 %copy-start = (f32[512,1024]{1,0:T(8,128)}, f32[512,1024]{1,0:T(8,128)S(1)}, u32[]{:S(2)}) copy-start(f32[512,1024]{1,0:T(8,128)S(1)} %fusion) | copy-start | bytes 6291460
  131.0 2.3 %copy-start.3 = (f32[512,1024]{1,0:T(8,128)S(1)}, f32[512,1024]{1,0:T(8,128)}, u32[]{:S(2)}) copy-start(f32[512,1024]{1,0:T(8,128)} %get-tuple-element.18) | copy-start | bytes 6291460
  133.4 3.3 %copy-start.2 = (f32[512,512]{1,0:T(8,128)}, f32[512,512]{1,0:T(8,128)S(1)}, u32[]{:S(2)}) copy-start(f32[512,512]{1,0:T(8,128)S(1)} %fusion.1) | copy-start | bytes 3145732

commit v4 on v3

--- a/solution.py
+++ b/solution.py
@@ -364,7 +364,7 @@
         fp[j, c] = x_ref[j, c]
         return copies
 
-    def route(j, copies):
+    def select_rows(j, copies):
         wait_all(copies)
 
         def four(n, carry):
@@ -379,6 +379,8 @@
             return carry
 
         lax.fori_loop(0, NC // 4, four, 0)
+
+    def send_rows(j):
         sends = to_rt(lambda t: routed.at[j, t], fs_ref.at[j, r], t2s.at[j], t2r.at[j])
         fs_ref[j, r] = routed[j, r]
         return sends
@@ -439,18 +441,34 @@
         r, c, g1s, g1r, g2s, g2r,
     )
 
+    def product(n, carry):
+        i = n // QUARTERS
+        j = lax.rem(n, QUARTERS)
+        ah, al = two_parts(apt[pl.ds(pl.multiple_of(i * LANES, LANES), LANES), :])
+        bh, bl = two_parts(fp[j].reshape(NC * SRC, QCOLS))
+        y = jnp.dot(ah, bh, preferred_element_type=f32)
+        y = y + jnp.dot(ah, bl, preferred_element_type=f32)
+        y = y + jnp.dot(al, bh, preferred_element_type=f32)
+        y = y.reshape(LANES // SLICE, SLICE, QCOLS)
+        at = pl.ds(lax.rem(i, 2) * (LANES // SLICE), LANES // SLICE)
+        part[i // 2, at, :, pl.ds(pl.multiple_of(j * QCOLS, QCOLS), QCOLS)] = y
+        return carry
+
+    columns = [start_columns(0)]
     panel.start()
     ap[c] = pan_ref[...]
-    columns = [start_columns(0)]
-    panel.forward()
     selections()
-    columns.append(start_columns(1))
-    panel.finish()
-    columns.append(start_columns(2))
-    columns.append(start_columns(3))
     po[...] = jnp.dot(
         sel_ref[c], three_parts(pan_ref[...]), preferred_element_type=f32
     ).reshape(NR, CAP, PANEL)
+    chunks = to_rt(lambda t: po.at[t], chunk.at[r], p1s, p1r)
+    chunk[r] = po[r]
+    panel.forward()
+    columns.append(start_columns(1))
+    select_rows(0, columns[0])
+    routes = [send_rows(0)]
+    columns.append(start_columns(2))
+    panel.finish()
     whole = ap[...].reshape(NC * SRC, PANEL)
     apt[...] = whole.T
     for i in range(PANEL // LANES):
@@ -465,10 +483,10 @@
             gpart[:, PAIRS.index((i, j))] = piece.reshape(NC, SUB, LANES)
     gram_sends = to_rt(lambda t: gpart.at[c], gin.at[r], p3s, p3r)
     gin[r] = gpart[c]
-    chunks = to_rt(lambda t: po.at[t], chunk.at[r], p1s, p1r)
-    chunk[r] = po[r]
-
-    routes = [route(0, columns[0])]
+    columns.append(start_columns(3))
+    select_rows(1, columns[1])
+    routes.append(send_rows(1))
+    make_perm()
     wait_all(gram_sends)
     total = gin[0]
     for t in range(1, NR):
@@ -476,47 +494,31 @@
     gsum[...] = total
     grams.start()
     gbuf[c] = total
-    routes.append(route(1, columns[1]))
+    select_rows(2, columns[2])
+    routes.append(send_rows(2))
+    order_columns(0, routes[0])
+    select_rows(3, columns[3])
+    lax.fori_loop(0, QUARTERS * (PANEL // LANES), product, 0)
+    swap = send(part.at[1 - core], ain, sa, ra, sibling, c)
     grams.forward()
     wait_all(chunks)
     rows.start()
     as_ref[:, c] = chunk[...]
-    routes.append(route(2, columns[2]))
+    swap.wait()
+    half[...] = part[core] + ain[...]
+    spread = [
+        send(half.at[peer // 2], bin_ref.at[d], sb.at[d], rb.at[d], peer, c)
+        for d, peer in enumerate(chip_peers)
+    ]
+    order_columns(1, routes[1])
     grams.finish()
     for n, (i, j) in enumerate(PAIRS):
         work[i * LANES : (i + 1) * LANES, j * LANES : (j + 1) * LANES] = gbuf[:, n].reshape(LANES, LANES)
     ids = lax.broadcasted_iota(jnp.int32, (PANEL, PANEL), 0)
     lanes = lax.broadcasted_iota(jnp.int32, (PANEL, PANEL), 1)
     work[:, PANEL:] = jnp.where(ids == lanes, 1.0, 0.0).astype(f32)
-    routes.append(route(3, columns[3]))
-    rows.forward()
-
-    def product(n, carry):
-        i = n // QUARTERS
-        j = lax.rem(n, QUARTERS)
-        ah, al = two_parts(apt[pl.ds(pl.multiple_of(i * LANES, LANES), LANES), :])
-        bh, bl = two_parts(fp[j].reshape(NC * SRC, QCOLS))
-        y = jnp.dot(ah, bh, preferred_element_type=f32)
-        y = y + jnp.dot(ah, bl, preferred_element_type=f32)
-        y = y + jnp.dot(al, bh, preferred_element_type=f32)
-        y = y.reshape(LANES // SLICE, SLICE, QCOLS)
-        at = pl.ds(lax.rem(i, 2) * (LANES // SLICE), LANES // SLICE)
-        part[i // 2, at, :, pl.ds(pl.multiple_of(j * QCOLS, QCOLS), QCOLS)] = y
-        return carry
-
-    lax.fori_loop(0, QUARTERS * (PANEL // LANES), product, 0)
-    swap = send(part.at[1 - core], ain, sa, ra, sibling, c)
-
     factor_step(0, work, small)
-    swap.wait()
-    half[...] = part[core] + ain[...]
-    spread = [
-        send(half.at[peer // 2], bin_ref.at[d], sb.at[d], rb.at[d], peer, c)
-        for d, peer in enumerate(chip_peers)
-    ]
-    make_perm()
     factor_step(1, work, small)
-    order_columns(0, routes[0])
     wait_all(spread)
     mine[...] = (half[x] + bin_ref[0]) + (bin_ref[1] + bin_ref[2])
     spread = [
@@ -524,15 +526,17 @@
     ]
     last = [send(mine, full.at[core, x], sd.at[CHIPS - 1], rd.at[CHIPS - 1], sibling, c)]
     full[core, x] = mine[...]
+    routes.append(send_rows(3))
+    rows.forward()
     factor_step(2, work, small)
-    factor_step(3, work, small)
-    inv_ref[...] = work[:, PANEL:]
     for d, copy in enumerate(spread):
         copy.wait()
         owner = lax.rem(x + CHIPS - d - 1, CHIPS)
         last.append(
             send(full.at[core, owner], full.at[core, owner], sd.at[d], rd.at[d], sibling, c)
         )
+    factor_step(3, work, small)
+    inv_ref[...] = work[:, PANEL:]
     rows.finish()
 
     def store_rows(lane_at):
@@ -544,10 +548,10 @@
     for n in range(PANEL // QCOLS):
         at = slice(n * QCOLS, (n + 1) * QCOLS)
         order(lambda t: as_ref[t].reshape(NC * CAP, PANEL)[:, at], store_rows(n * QCOLS), QCOLS)
-    for j in range(1, QUARTERS):
-        order_columns(j, routes[j])
+    order_columns(2, routes[2])
     wait_all(last)
     sum_ref[...] = full[...].reshape(PANEL, BLOCK_COLS)
+    order_columns(3, routes[3])
 
 
 def factor_step(b, work, small):

time: 137 us -> 125 us (0.912)
  Pallas kernels: 126 us -> 114 us
    pallas_call x1, Pallas kernels: 117 us -> 104 us  [build_front(): pl.pallas_call(front_kernel, in_specs=[pl.BlockSpec(memory_space=pltpu.VM...]
where the time goes in v4:
time: 125 us
  Pallas kernels  114 us (91%)
  matrix products  8.31 us (7%)
  local copies, waits for them, and re-layouts  1.29 us (1%)
    pallas_call x1, Pallas kernels, build_front(): pl.pallas_call(front_kernel, in_specs=[pl.BlockSpec(memory_space=pltpu.VM...  104 us
    pallas_call x1, Pallas kernels, place_columns(): pl.pallas_call(table_kernel, in_specs=[pl.BlockSpec(memory_space=pltpu.SM...  9.89 us
    dot_general x1, matrix products, shards(): jnp.dot(inverse, projected, precision=high, preferred_element_type=f32)  3.91 us
    dot_general x1, matrix products, shards(): lax.dot_general(basis, factor_rows, (((0,), (0,)), ((), ())), precision=h...  3.33 us

profile of v4, /device:TPU:0, one launch (start us, length us, event | category | flops | bytes accessed | tf_op | source)
XLA Modules:
  0.0 124.7 jit_solution(14425921677514096056)
XLA Ops:
  0.6 9.9 %shard_map.67 = (f32[4,16,32,256]{3,2,1,0:T(8,128)}, f32[32,512]{1,0:T(8,128)}, s32[32,128]{1,0:T(8,128)}, s32[8,1024]{1,0:T(8,128)}) custom-call(s32[2,48]{1,0:T(2,128)} %stair_ref.1, s32[32,128]{1,0:T(8,128)} %bitcast.7, s32[2,12288]{1,0:T(2,128)} %col_ref.1, f32[32,12288]{1,0:T(8,128)} %ch_ref.1), custom_call_target="tpu_custom_call" | custom-call | flops 400000000 | bytes 4000000 | tf_op jit(solution)/shard_map/pallas_call | solution.py:146
  10.5 104.5 %shard_map.68 = (f32[512,1024]{1,0:T(8,128)}, f32[512,512]{1,0:T(8,128)}, f32[512,1024]{1,0:T(8,128)}, f32[512,512]{1,0:T(8,128)}) custom-call(f32[4,16,32,256]{3,2,1,0:T(8,128)} %get-tuple-element.11.x_ref, f32[32,512]{1,0:T(8,128)} %get-tuple-element.12.pan_ref, s32[32,128]{1,0:T(8,128)} %get-tuple-element.13.slot_ref, s32[8,1024]{1,0:T(8,128)} %get-tuple-element.14.order_ref), custom_call_target="tpu_custom_call" | custom-call | flops 3000000000 | bytes 300000000 | tf_op jit(solution)/shard_map/pallas_call | solution.py:586
  115.0 0.0 copy-start.1
  115.0 0.0 copy-start.4
  115.0 3.9 %fusion = f32[512,1024]{1,0:T(8,128)S(1)} fusion(f32[512,512]{1,0:T(8,128)} %get-tuple-element.15, f32[512,1024]{1,0:T(8,128)} %get-tuple-element.16), kind=kOutput, calls=%fused_computation.1 | convolution fusion | flops 1610612736 | bytes 5242880 | tf_op jit(solution)/shard_map/dot_general | solution.py:653
  119.0 0.0 copy-done.1
  119.0 0.0 copy-done.4
  119.0 0.0 copy-start
  119.0 0.0 copy-start.3
  119.0 1.1 fusion.1
  120.1 1.3 %copy-done.3 = f32[512,1024]{1,0:T(8,128)S(1)} copy-done((f32[512,1024]{1,0:T(8,128)S(1)}, f32[512,1024]{1,0:T(8,128)}, u32[]{:S(2)}) %copy-start.3) | copy-done | bytes 2097176
  121.3 0.0 copy-start.2
  121.3 3.3 %convolution_subtract_fusion = f32[512,1024]{1,0:T(8,128)} fusion(f32[512,1024]{1,0:T(8,128)S(1)} %copy-done.3, f32[512,512]{1,0:T(8,128)S(1)} %fusion.1, f32[512,1024]{1,0:T(8,128)S(1)} %fusion), kind=kOutput, calls=%fused_computation | convolution fusion | flops 1611137024 | bytes 7340032 | tf_op jit(solution)/shard_map/dot_general | solution.py:654
  124.7 0.0 copy-done
  124.7 0.0 copy-done.2
Async XLA Ops:
  115.0 3.9 %copy-start.1 = (f32[512,512]{1,0:T(8,128)S(1)}, f32[512,512]{1,0:T(8,128)}, u32[]{:S(2)}) copy-start(f32[512,512]{1,0:T(8,128)} %get-tuple-element.15) | copy-start | bytes 3145732
  115.0 3.9 %copy-start.4 = (f32[512,512]{1,0:T(8,128)S(1)}, f32[512,512]{1,0:T(8,128)}, u32[]{:S(2)}) copy-start(f32[512,512]{1,0:T(8,128)} %get-tuple-element.17) | copy-start | bytes 3145732
  119.0 5.7 %copy-start = (f32[512,1024]{1,0:T(8,128)}, f32[512,1024]{1,0:T(8,128)S(1)}, u32[]{:S(2)}) copy-start(f32[512,1024]{1,0:T(8,128)S(1)} %fusion) | copy-start | bytes 6291460
  119.0 2.3 %copy-start.3 = (f32[512,1024]{1,0:T(8,128)S(1)}, f32[512,1024]{1,0:T(8,128)}, u32[]{:S(2)}) copy-start(f32[512,1024]{1,0:T(8,128)} %get-tuple-element.18) | copy-start | bytes 6291460
  121.3 3.3 %copy-start.2 = (f32[512,512]{1,0:T(8,128)}, f32[512,512]{1,0:T(8,128)S(1)}, u32[]{:S(2)}) copy-start(f32[512,512]{1,0:T(8,128)S(1)} %fusion.1) | copy-start | bytes 3145732

commit v5 on v4

--- a/solution.py
+++ b/solution.py
@@ -22,6 +22,8 @@
 QUARTERS = 4
 QCOLS = BLOCK_COLS // QUARTERS
 SIDE = 4
+COLUMN_ORDER = (1, 15, 4, 12, 5, 11, 3, 13, 8, 2, 14, 6, 10, 7, 9)
+ROW_ORDER = (2, 6, 3, 5, 4, 7, 1)
 CHIPS = NR // 2
 SLICE = PANEL // NR
 PAIRS = [(i, j) for i in range(PANEL // LANES) for j in range(i, PANEL // LANES)]
@@ -331,7 +333,7 @@
 
     def to_rt(src_of, dst, ss, rs):
         copies = []
-        for d in range(1, NR):
+        for d in ROW_ORDER:
             t = lax.rem(r + d, NR)
             copies.append(send(src_of(t), dst, ss.at[d - 1], rs.at[d - 1], t, c))
         return copies
@@ -356,7 +358,7 @@
 
     def start_columns(j):
         copies = []
-        for e in range(1, NC):
+        for e in COLUMN_ORDER:
             to = lax.rem(c + e, NC)
             copies.append(
                 send(x_ref.at[j, to], fp.at[j, c], t1s.at[j, e - 1], t1r.at[j, e - 1], r, to)
@@ -389,10 +391,9 @@
         def split(n, carry):
             at = pl.ds(pl.multiple_of(n * LANES, LANES), LANES)
             rest = load(n)
-            for p in range(3):
-                piece = rest.astype(bf16)
-                parts[p, at, :width] = piece
-                rest = rest - piece.astype(f32)
+            hi, lo = two_parts(rest)
+            parts[0, at, :width] = hi
+            parts[1, at, :width] = lo
             return carry
 
         lax.fori_loop(0, NR, split, 0)
@@ -401,7 +402,6 @@
             at = pl.ds(pl.multiple_of(n * LANES, LANES), LANES)
             y = jnp.dot(perm[at, :], parts[0, :, :width], preferred_element_type=f32)
             y = y + jnp.dot(perm[at, :], parts[1, :, :width], preferred_element_type=f32)
-            y = y + jnp.dot(perm[at, :], parts[2, :, :width], preferred_element_type=f32)
             store(at, y)
             return carry
 
@@ -598,7 +598,7 @@
             vmem((QUARTERS, NR, slots, QCOLS), f32),
             vmem((NR, NC, CAP, PANEL), f32),
             vmem((ROWS_DEV, NR * slots), bf16),
-            vmem((3, NR * slots, QCOLS), bf16),
+            vmem((2, NR * slots, QCOLS), bf16),
             vmem((NR, CAP, PANEL), f32),
             vmem((NR, CAP, PANEL), f32),
             vmem((NC, SRC, PANEL), f32),

time: 125 us -> 124 us (level); the launches traced: 125 us -> 122 us
  Pallas kernels: 114 us -> 111 us
    pallas_call x1, Pallas kernels: 104 us -> 101 us  [build_front(): pl.pallas_call(front_kernel, in_specs=[pl.BlockSpec(memory_space=pltpu.VM...]
where the time goes in v5:
time: 124 us; the launch traced here: 122 us
  Pallas kernels  111 us (90%)
  matrix products  8.31 us (7%)
  local copies, waits for them, and re-layouts  1.29 us (1%)
    pallas_call x1, Pallas kernels, build_front(): pl.pallas_call(front_kernel, in_specs=[pl.BlockSpec(memory_space=pltpu.VM...  101 us
    pallas_call x1, Pallas kernels, place_columns(): pl.pallas_call(table_kernel, in_specs=[pl.BlockSpec(memory_space=pltpu.SM...  9.89 us
    dot_general x1, matrix products, shards(): jnp.dot(inverse, projected, precision=high, preferred_element_type=f32)  3.91 us
    dot_general x1, matrix products, shards(): lax.dot_general(basis, factor_rows, (((0,), (0,)), ((), ())), precision=h...  3.33 us

profile of v5, /device:TPU:0, one launch (start us, length us, event | category | flops | bytes accessed | tf_op | source)
XLA Modules:
  0.0 121.6 jit_solution(14015852048004564218)
XLA Ops:
  0.6 9.9 %shard_map.67 = (f32[4,16,32,256]{3,2,1,0:T(8,128)}, f32[32,512]{1,0:T(8,128)}, s32[32,128]{1,0:T(8,128)}, s32[8,1024]{1,0:T(8,128)}) custom-call(s32[2,48]{1,0:T(2,128)} %stair_ref.1, s32[32,128]{1,0:T(8,128)} %bitcast.7, s32[2,12288]{1,0:T(2,128)} %col_ref.1, f32[32,12288]{1,0:T(8,128)} %ch_ref.1), custom_call_target="tpu_custom_call" | custom-call | flops 400000000 | bytes 4000000 | tf_op jit(solution)/shard_map/pallas_call | solution.py:148
  10.5 101.4 %shard_map.68 = (f32[512,1024]{1,0:T(8,128)}, f32[512,512]{1,0:T(8,128)}, f32[512,1024]{1,0:T(8,128)}, f32[512,512]{1,0:T(8,128)}) custom-call(f32[4,16,32,256]{3,2,1,0:T(8,128)} %get-tuple-element.11.x_ref, f32[32,512]{1,0:T(8,128)} %get-tuple-element.12.pan_ref, s32[32,128]{1,0:T(8,128)} %get-tuple-element.13.slot_ref, s32[8,1024]{1,0:T(8,128)} %get-tuple-element.14.order_ref), custom_call_target="tpu_custom_call" | custom-call | flops 3000000000 | bytes 300000000 | tf_op jit(solution)/shard_map/pallas_call | solution.py:586
  112.0 0.0 copy-start.1
  112.0 0.0 copy-start.4
  112.0 3.9 %fusion = f32[512,1024]{1,0:T(8,128)S(1)} fusion(f32[512,512]{1,0:T(8,128)} %get-tuple-element.15, f32[512,1024]{1,0:T(8,128)} %get-tuple-element.16), kind=kOutput, calls=%fused_computation.1 | convolution fusion | flops 1610612736 | bytes 5242880 | tf_op jit(solution)/shard_map/dot_general | solution.py:653
  115.9 0.0 copy-done.1
  115.9 0.0 copy-done.4
  115.9 0.0 copy-start
  115.9 0.0 copy-start.3
  116.0 1.1 fusion.1
  117.0 1.3 %copy-done.3 = f32[512,1024]{1,0:T(8,128)S(1)} copy-done((f32[512,1024]{1,0:T(8,128)S(1)}, f32[512,1024]{1,0:T(8,128)}, u32[]{:S(2)}) %copy-start.3) | copy-done | bytes 2097176
  118.3 0.0 copy-start.2
  118.3 3.3 %convolution_subtract_fusion = f32[512,1024]{1,0:T(8,128)} fusion(f32[512,1024]{1,0:T(8,128)S(1)} %copy-done.3, f32[512,512]{1,0:T(8,128)S(1)} %fusion.1, f32[512,1024]{1,0:T(8,128)S(1)} %fusion), kind=kOutput, calls=%fused_computation | convolution fusion | flops 1611137024 | bytes 7340032 | tf_op jit(solution)/shard_map/dot_general | solution.py:654
  121.6 0.0 copy-done
  121.6 0.0 copy-done.2
Async XLA Ops:
  112.0 3.9 %copy-start.1 = (f32[512,512]{1,0:T(8,128)S(1)}, f32[512,512]{1,0:T(8,128)}, u32[]{:S(2)}) copy-start(f32[512,512]{1,0:T(8,128)} %get-tuple-element.15) | copy-start | bytes 3145732
  112.0 3.9 %copy-start.4 = (f32[512,512]{1,0:T(8,128)S(1)}, f32[512,512]{1,0:T(8,128)}, u32[]{:S(2)}) copy-start(f32[512,512]{1,0:T(8,128)} %get-tuple-element.17) | copy-start | bytes 3145732
  115.9 5.7 %copy-start = (f32[512,1024]{1,0:T(8,128)}, f32[512,1024]{1,0:T(8,128)S(1)}, u32[]{:S(2)}) copy-start(f32[512,1024]{1,0:T(8,128)S(1)} %fusion) | copy-start | bytes 6291460
  115.9 2.3 %copy-start.3 = (f32[512,1024]{1,0:T(8,128)S(1)}, f32[512,1024]{1,0:T(8,128)}, u32[]{:S(2)}) copy-start(f32[512,1024]{1,0:T(8,128)} %get-tuple-element.18) | copy-start | bytes 6291460
  118.3 3.3 %copy-start.2 = (f32[512,512]{1,0:T(8,128)}, f32[512,512]{1,0:T(8,128)S(1)}, u32[]{:S(2)}) copy-start(f32[512,512]{1,0:T(8,128)S(1)} %fusion.1) | copy-start | bytes 3145732
